TPU v7x, 512 devices: a whole 4x8x8 slice. The times are simulated.
512 devices in a mesh: row: 32 (over z_lo, x, core), col: 16 (over y, z_hi).
Axes of the slice: x: 4, y: 8, z: 8 (z_hi: 2, z_lo: 4; z = z_hi * 4 + z_lo), core: 2. Of those that a mesh axis runs over, the one named last changes fastest.
Arguments:
- halves: bfloat16 [96, 800, 800], P(None, 'row', 'col'), may hold values from -6 to 6
- first_factor: bfloat16 [4000, 800], P('col'), may hold values from -0.21875 to 0.21875
- second_factor: bfloat16 [4000, 800], P('col'), may hold values from -0.09375 to 0.09375
- weights: bfloat16 [4000, 96], P('col'), may hold values from 0.25 to 4
Outputs:
- cycle: bfloat16 [96, 800, 800], P('col', 'row')
All inputs are finite; a program needn't handle non-finite values.
Results may differ from a plain program's by a relative error of at most 0.0095.
Values may be sent and summed in bfloat16 or wider, within the bound.
No kernel may reach another device: no remote copies, remote signals or barrier semaphores. Data moves between devices by JAX's collectives and lax.ppermute only.
A program may use at most 64 MiB of HBM per device.

v0:
```python
import jax
import jax.numpy as jnp
from jax import lax
from jax.sharding import PartitionSpec as P


def body(halves, first_factor, second_factor, weights):
    regrouped = lax.all_to_all(halves, "col", split_axis=0, concat_axis=2, tiled=True)
    mirrored = lax.all_to_all(regrouped, "row", split_axis=2, concat_axis=1, tiled=True)
    amplitude = (
        regrouped.astype(jnp.float32) - jnp.swapaxes(mirrored, 1, 2).astype(jnp.float32)
    ).astype(jnp.bfloat16)
    own_count, row_count, virtual_count = amplitude.shape
    block_size = first_factor.shape[0]
    first_index = lax.axis_index("col") * own_count
    first_piece = lax.all_gather(first_factor, "col", axis=0, tiled=True)
    second_piece = lax.all_gather(second_factor, "col", axis=0, tiled=True)
    scale_piece = lax.all_gather(weights, "col", axis=0, tiled=True)
    block_count = first_piece.shape[0] // block_size
    chosen = lax.dynamic_slice_in_dim(scale_piece, first_index, own_count, 1)
    scaled = jnp.einsum("iab,qb->iaq", amplitude, first_piece, preferred_element_type=jnp.float32)
    scaled = scaled * jnp.transpose(chosen).astype(jnp.float32)[:, None, :]
    scaled = scaled.astype(jnp.bfloat16).reshape(own_count, row_count, block_count, block_size)
    blocks = jnp.einsum(
        "iakq,kqc->kiac",
        scaled,
        second_piece.reshape(block_count, block_size, virtual_count),
        preferred_element_type=jnp.float32,
    )
    blocks = lax.optimization_barrier(blocks.astype(jnp.bfloat16)).astype(jnp.float32)
    summed = jnp.sum(blocks, axis=0)
    return summed.astype(jnp.bfloat16)


def solution(mesh):
    placed = (P(None, "row", "col"), P("col", None), P("col", None), P("col", None))
    return jax.shard_map(
        body, mesh=mesh, in_specs=placed, out_specs=P("col", "row", None), check_vma=False
    )
```

profile of v0, /device:TPU:1, one launch (start us, length us, event | category | flops | bytes accessed | tf_op | source)
XLA Modules:
  0.0 381.4 jit_solution(3163894563325120235)
XLA Ops:
  6.5 0.0 all-gather.6.cloned.1.call-start
  6.5 0.7 all-gather.6.cloned.1.call-update
  7.3 0.0 copy-start.1
  7.3 0.0 all-gather.8.cloned.1.call-start
  7.3 0.7 all-gather.8.cloned.1.call-update
  8.0 2.1 copy.20
  10.2 1.2 reshape.25
  11.4 30.2 %all_to_all.27 = bf16[16,2,3750]{2,1,0:T(2,128)(2,1)S(1)} all-to-all(bf16[16,2,3750]{2,1,0:T(2,128)(2,1)S(1)} %reshape.25), channel_id=1, replica_groups=mesh['row'=32,'col'=16] {'col'}, dimensions={0} | all-to-all | bytes 480000 | tf_op jit(solution)/shard_map/all_to_all | solution.py:8
  41.5 1.7 reshape.26
  43.2 0.4 copy.22
  43.6 0.7 all_to_all.23
  44.4 2.1 copy.23
  46.4 2.2 reshape.27
  48.6 11.9 %all-to-all-start.1 = ((bf16[32,2,1875]{2,1,0:T(2,128)(2,1)}), bf16[32,2,1875]{2,1,0:T(2,128)(2,1)S(1)}, u32[]{:S(2)}, u32[]{:S(2)}) async-start(bf16[32,2,1875]{2,1,0:T(2,128)(2,1)} %reshape.27), calls=%async_computation.1 | async-start | bytes 491520 | tf_op jit(solution)/shard_map/all_to_all | solution.py:9
  60.6 0.0 copy-done.1
  60.6 67.8 %all-gather.1 = bf16[16,250,96]{1,2,0:T(8,128)(2,1)S(1)} all-gather(bf16[1,250,96]{1,2,0:T(8,128)(2,1)S(1)} %bitcast.45), channel_id=1, replica_groups=mesh['row'=32,'col'=16] {'col'}, dimensions={0}, use_global_device_ids=true | all-gather | bytes 816000 | tf_op jit(solution)/shard_map/all_gather | solution.py:18
  128.4 0.4 copy.26
  128.8 1.3 reshape.18
  130.1 0.0 all-to-all-done.1
  130.2 2.8 reshape.28
  132.9 1.8 copy.34
  134.7 3.1 reshape.13
  137.7 63.6 %all-gather.6.cloned.1.call-done = bf16[16,250,800]{1,2,0:T(8,128)(2,1)} async-done(((bf16[1,250,800]{1,2,0:T(8,128)(2,1)}), bf16[16,250,800]{1,2,0:T(8,128)(2,1)}) %all-gather.6.cloned.1.call-update) | async-done | bytes 6400016 | tf_op jit(solution)/shard_map/all_gather | solution.py:16
  201.4 9.2 %copy.25 = bf16[16,250,800]{1,0,2:T(8,128)(2,1)} copy(bf16[16,250,800]{1,2,0:T(8,128)(2,1)} %all-gather.6.cloned.1.call-done) | data formatting | bytes 12800000 | tf_op jit(solution)/shard_map/all_gather | solution.py:16
  210.6 0.0 copy-start
  210.6 14.3 %reshape.22 = bf16[4000,800,1]{0,1,2:T(8,128)(2,1)} reshape(bf16[16,250,800]{1,0,2:T(8,128)(2,1)} %copy.25) | data formatting | bytes 12800000
  224.9 0.0 copy-done
  224.9 4.7 %fusion.2 = bf16[6,25,4000]{2,1,0:T(8,128)(2,1)S(1)} fusion(bf16[4000,800,1]{0,1,2:T(8,128)(2,1)} %reshape.22, f32[6,4000]{1,0:T(8,128)S(1)} %convert_bitcast_fusion, f32[6,800,25]{1,2,0:T(8,128)S(1)} %copy-done, bf16[6,25,800]{2,1,0:T(8,128)(2,1)S(1)} %all_to_all.23), kind=kOutput, calls=%fused_computation.3 | convolution fusion | flops 961560000 | bytes 8416000 | tf_op jit(solution)/shard_map/iab,qb->iaq/dot_general | solution.py:21
  229.6 4.1 %reshape.11 = bf16[6,25,16,250]{3,2,1,0:T(8,128)(2,1)S(1)} reshape(bf16[6,25,4000]{2,1,0:T(8,128)(2,1)S(1)} %fusion.2) | data formatting | bytes 2400000 | tf_op jit(solution)/shard_map/reshape | solution.py:23
  233.7 128.9 %all-gather.8.cloned.1.call-done = bf16[16,250,800]{1,2,0:T(8,128)(2,1)} async-done(((bf16[1,250,800]{1,2,0:T(8,128)(2,1)}), bf16[16,250,800]{1,2,0:T(8,128)(2,1)}) %all-gather.8.cloned.1.call-update) | async-done | bytes 6400016 | tf_op jit(solution)/shard_map/all_gather | solution.py:17
  362.6 7.6 %fusion.3 = bf16[16,6,25,800]{3,2,1,0:T(8,128)(2,1)} fusion(bf16[16,250,800]{1,2,0:T(8,128)(2,1)} %all-gather.8.cloned.1.call-done, bf16[6,25,16,250]{3,2,1,0:T(8,128)(2,1)S(1)} %reshape.11), kind=kOutput, calls=%fused_computation.4 | convolution fusion | flops 961920000 | bytes 11440000 | tf_op jit(solution)/shard_map/iakq,kqc->kiac/dot_general | solution.py:24
  370.3 4.3 %reduce_sum.12 = bf16[6,25,800]{2,1,0:T(8,128)(2,1)} reduce(bf16[16,6,25,800]{3,2,1,0:T(8,128)(2,1)} %fusion.3, bf16[]{:T(256)} %constant.12.clone.1), dimensions={0}, to_apply=%region_0.0 | reduce | flops 1800000 | bytes 4080002 | tf_op jit(solution)/shard_map/reduce_sum | solution.py:31
  (1 shorter events, 0.0 us)
Async XLA Ops:
  6.5 194.8 %all-gather.6.cloned.1.call-start = ((), (), s32[]{:S(2)}) async-start(), calls=%async_computation.2 | async-start | bytes 6963200 | tf_op jit(solution)/shard_map/all_gather | solution.py:16
  7.3 53.3 %copy-start.1 = (bf16[250,96]{0,1:T(8,128)(2,1)S(1)}, bf16[250,96]{0,1:T(8,128)(2,1)}, u32[]{:S(2)}) copy-start(bf16[250,96]{0,1:T(8,128)(2,1)} %param.7) | copy-start | bytes 144004
  7.3 355.4 %all-gather.8.cloned.1.call-start = ((), (), s32[]{:S(2)}) async-start(), calls=%async_computation.3 | async-start | bytes 6963200 | tf_op jit(solution)/shard_map/all_gather | solution.py:17
  48.6 81.5 %all-to-all-start.1 = ((bf16[32,2,1875]{2,1,0:T(2,128)(2,1)}), bf16[32,2,1875]{2,1,0:T(2,128)(2,1)S(1)}, u32[]{:S(2)}, u32[]{:S(2)}) async-start(bf16[32,2,1875]{2,1,0:T(2,128)(2,1)} %reshape.27), calls=%async_computation.1 | async-start | bytes 491520 | tf_op jit(solution)/shard_map/all_to_all | solution.py:9
  210.6 14.3 %copy-start = (f32[6,800,25]{1,2,0:T(8,128)S(1)}, f32[6,800,25]{1,2,0:T(8,128)}, u32[]{:S(2)}) copy-start(f32[6,800,25]{1,2,0:T(8,128)} %reshape.13) | copy-start | bytes 1440004
Sparse Core Ops, SparseCore 0:
  10.5 190.8 all-gather.5
  204.6 158.0 all-gather.7
where the time goes:
time: 385 us; the launch traced here: 381 us
  waiting for transfers between devices  194 us (50%)
  blocking collectives  98 us (25%)
  local copies, waits for them, and re-layouts  47.3 us (12%)
  between operations  13.5 us (4%)
  matrix products  12.3 us (3%)
  starting transfers between devices  12 us (3%)
  other arithmetic  4.32 us (1%)
    all_gather x1, waiting for transfers between devices, body(): second_piece = lax.all_gather(second_factor, 'col', axis=0, tiled=True)  129 us
    all_gather x1, blocking collectives, body(): scale_piece = lax.all_gather(weights, 'col', axis=0, tiled=True)  67.8 us
    all_gather x1, waiting for transfers between devices, body(): first_piece = lax.all_gather(first_factor, 'col', axis=0, tiled=True)  63.6 us
    all_to_all x1, blocking collectives, body(): lax.all_to_all(halves, 'col', split_axis=0, concat_axis=2, tiled=True)  30.2 us
    unnamed x11, local copies, waits for them, and re-layouts  25.5 us
    all_to_all x1, starting transfers between devices, body(): lax.all_to_all(regrouped, 'row', split_axis=2, concat_axis=1, tiled=True)  11.9 us
    all_gather x1, local copies, waits for them, and re-layouts, body(): first_piece = lax.all_gather(first_factor, 'col', axis=0, tiled=True)  9.25 us
  transfers between devices with their start and end apart: 3, of which 2 were waited for; matrix products, arithmetic and copies ran while one was open for 13% of the time, Pallas kernels for 0%

commit v1 on v0

v1 whole, which is shorter than its diff:
```python
import functools

import jax
import jax.numpy as jnp
from jax import lax
from jax.experimental import pallas as pl
from jax.experimental.pallas import tpu as pltpu
from jax.sharding import Mesh, PartitionSpec as P

ROWS, SLOT, LANES = 25, 32, 128


def amplitude_kernel(direct_ref, mirrored_ref, out_ref):
    count = mirrored_ref.shape[0]
    mirrored = mirrored_ref[...].astype(jnp.float32).reshape(count * SLOT, LANES)
    mirrored = jnp.transpose(mirrored)
    lane = lax.broadcasted_iota(jnp.int32, (SLOT, LANES), 1) // SLOT
    for quad in range(count // 4):
        parts = [direct_ref[quad, k].astype(jnp.float32) for k in range(4)]
        for orbital in range(4):
            direct = None
            for k in range(4):
                shift = SLOT * ((k - orbital) % 4)
                moved = pltpu.roll(parts[k], shift, 1) if shift else parts[k]
                direct = moved if direct is None else jnp.where(lane == k, moved, direct)
            rows = slice(orbital * SLOT, (orbital + 1) * SLOT)
            columns = slice(quad * LANES, (quad + 1) * LANES)
            out_ref[rows, columns] = (direct - mirrored[rows, columns]).astype(out_ref.dtype)


def contraction_kernel(where_ref, amplitude_ref, factors_ref, own_ref, other_ref, total_ref, *, orbitals):
    step = pl.program_id(0)
    rows, depth = amplitude_ref.shape
    virtual = own_ref.shape[1]
    pick = lax.broadcasted_iota(jnp.int32, (rows, orbitals), 0) // SLOT + where_ref[0]
    pick = (pick == lax.broadcasted_iota(jnp.int32, (rows, orbitals), 1)).astype(jnp.bfloat16)
    scaled = jnp.dot(amplitude_ref[...], factors_ref[0, :depth], preferred_element_type=jnp.float32)
    scale = jnp.dot(pick, factors_ref[0, depth : depth + orbitals], preferred_element_type=jnp.float32)
    scaled = (scaled * scale).astype(jnp.bfloat16)
    part = lax.dot_general(
        scaled, factors_ref[0, depth + orbitals :], (((1,), (1,)), ((), ())), preferred_element_type=jnp.float32
    )

    @pl.when(step == 0)
    def _():
        total_ref[...] = part

    @pl.when(step > 0)
    def _():
        total_ref[...] += part

    @pl.when(step == pl.num_programs(0) - 1)
    def _():
        half = rows // 2
        mine = where_ref[1]
        own_ref[...] = total_ref[pl.ds(pl.multiple_of(mine * half, half), half), :]
        other_ref[...] = total_ref[pl.ds(pl.multiple_of((1 - mine) * half, half), half), :].astype(other_ref.dtype)


def body(halves, first_factor, second_factor, weights):
    y_count, row_count = lax.axis_size("y"), lax.axis_size("p") * 2
    orbitals, block = halves.shape[0], first_factor.shape[0]
    virtual = first_factor.shape[1]
    local = orbitals // y_count
    groups = local // 4
    y, zh, core = lax.axis_index("y"), lax.axis_index("zh"), lax.axis_index("c")

    lanes = (block + LANES - 1) // LANES * LANES
    widen = ((0, 0), (0, lanes - block))
    first = jnp.pad(first_factor.T.reshape(row_count, ROWS, block), ((0, 0), (0, SLOT - ROWS), (0, lanes - block)))
    packed = jnp.concatenate(
        [first.reshape(row_count * SLOT, lanes), jnp.pad(weights.T, widen), jnp.pad(second_factor.T, widen)]
    )
    half = packed.shape[0] // 2
    share = lax.dynamic_slice_in_dim(packed, core * half, half, 0)
    factors = lax.all_gather(share, ("y", "c"), axis=0, tiled=True).reshape(y_count, 2 * half, lanes)

    pieces = halves.reshape(y_count, groups, 4, ROWS, 2, ROWS).transpose(0, 4, 1, 3, 2, 5)
    slack = (0, SLOT - ROWS)
    pieces = jnp.pad(pieces, ((0, 0), (0, 0), (0, 0), slack, (0, 0), slack))
    pieces = pieces.reshape(y_count, 1, 2, groups * SLOT, LANES)
    pieces = jnp.broadcast_to(pieces, (y_count, 2, 2, groups * SLOT, LANES)).reshape(2 * y_count, 2, groups * SLOT, LANES)
    direct = lax.all_to_all(pieces, ("y", "zh"), 0, 0, tiled=True).reshape(row_count, groups * SLOT, LANES)
    mirrored = lax.all_to_all(direct, ("p", "c"), 0, 0, tiled=True)
    amplitude = pl.pallas_call(
        amplitude_kernel,
        grid=(groups,),
        in_specs=[
            pl.BlockSpec((row_count // 4, 4, SLOT, LANES), lambda g: (0, 0, g, 0)),
            pl.BlockSpec((row_count, SLOT, LANES), lambda g: (0, g, 0)),
        ],
        out_specs=pl.BlockSpec((LANES, row_count * SLOT), lambda g: (g, 0)),
        out_shape=jax.ShapeDtypeStruct((groups * LANES, row_count * SLOT), jnp.bfloat16),
        name="amplitude",
    )(direct.reshape(row_count // 4, 4, groups * SLOT, LANES), mirrored)

    rows = local * SLOT
    where = jnp.stack([y * local, zh])
    own, other = pl.pallas_call(
        functools.partial(contraction_kernel, orbitals=orbitals),
        grid=(y_count,),
        in_specs=[
            pl.BlockSpec(memory_space=pltpu.SMEM),
            pl.BlockSpec((rows, row_count * SLOT), lambda k: (0, 0)),
            pl.BlockSpec((1, 2 * half, lanes), lambda k: (k, 0, 0)),
        ],
        out_specs=[pl.BlockSpec((rows // 2, virtual), lambda k: (0, 0))] * 2,
        out_shape=[
            jax.ShapeDtypeStruct((rows // 2, virtual), jnp.float32),
            jax.ShapeDtypeStruct((rows // 2, virtual), jnp.bfloat16),
        ],
        scratch_shapes=[pltpu.VMEM((rows, virtual), jnp.float32)],
        name="contraction",
    )(where, amplitude, factors)
    received = lax.ppermute(other, "zh", [(0, 1), (1, 0)])
    cycle = (own + received.astype(jnp.float32)).astype(jnp.bfloat16)
    return cycle.reshape(local // 2, SLOT, virtual)[:, :ROWS]


def solution(mesh):
    rows, columns = mesh.devices.shape
    fine = Mesh(mesh.devices.reshape(rows // 2, 2, columns // 2, 2), ("p", "c", "y", "zh"))
    row, col = ("p", "c"), ("y", "zh")
    placed = (P(None, row, col), P(col, None), P(col, None), P(col, None))
    return jax.shard_map(body, mesh=fine, in_specs=placed, out_specs=P(col, row, None), check_vma=False)
```

time: 385 us -> 144 us (0.37)
  waiting for transfers between devices: 194 us -> 41 us
  blocking collectives: 98 us -> 50.1 us
  local copies, waits for them, and re-layouts: 47.3 us -> 5.23 us
  Pallas kernels: 0 us -> 15.3 us
  matrix products: 12.3 us -> 0 us
    all_gather x2 -> x1, waiting for transfers between devices: 193 us -> 0.01 us  [body(): lax.all_gather(share, ('y', 'c'), axis=0, tiled=True)]
    all_gather x1 -> x0, blocking collectives: 67.8 us -> none  [body(): scale_piece = lax.all_gather(weights, 'col', axis=0, tiled=True)]
    unnamed x11 -> x10, local copies, waits for them, and re-layouts: 25.5 us -> 1.58 us
    all_to_all x1, waiting for transfers between devices: 0.01 us -> 21 us  [body(): mirrored = lax.all_to_all(direct, ('p', 'c'), 0, 0, tiled=True)]
    all_to_all x1, blocking collectives: 30.2 us -> 50.1 us  [body(): lax.all_to_all(pieces, ('y', 'zh'), 0, 0, tiled=True)]
    ppermute x0 -> x1, waiting for transfers between devices: none -> 20 us  [body(): received = lax.ppermute(other, 'zh', [(0, 1), (1, 0)])]
    pallas_call x0 -> x2, Pallas kernels: none -> 15.3 us  [the longest x1 11.7 us: body(): pl.pallas_call(functools.partial(contraction_kernel, orbitals=orbitals),...]
    dot_general x2 -> x0, matrix products: 12.3 us -> none  [the longest x1 7.65 us: body(): jnp.einsum('iakq,kqc->kiac', scaled, second_piece.reshape(block_count, bl...]
  transfers between devices with their start and end apart: 3 -> 3, of which waited for: 2 -> 2; matrix products, arithmetic and copies ran while one was open for 13% -> 3% of each run, Pallas kernels for 0% -> 3%
where the time goes in v1:
time: 144 us; the launch traced here: 143 us
  blocking collectives  50.1 us (35%)
  waiting for transfers between devices  41 us (28%)
  Pallas kernels  15.3 us (11%)
  between operations  13.5 us (9%)
  starting transfers between devices  12.4 us (9%)
  other arithmetic  5.4 us (4%)
  local copies, waits for them, and re-layouts  5.23 us (4%)
    all_to_all x1, blocking collectives, body(): lax.all_to_all(pieces, ('y', 'zh'), 0, 0, tiled=True)  50.1 us
    all_to_all x1, waiting for transfers between devices, body(): mirrored = lax.all_to_all(direct, ('p', 'c'), 0, 0, tiled=True)  21 us
    ppermute x1, waiting for transfers between devices, body(): received = lax.ppermute(other, 'zh', [(0, 1), (1, 0)])  20 us
    pallas_call x1, Pallas kernels, body(): pl.pallas_call(functools.partial(contraction_kernel, orbitals=orbitals),...  11.7 us
    all_to_all x1, starting transfers between devices, body(): mirrored = lax.all_to_all(direct, ('p', 'c'), 0, 0, tiled=True)  10.5 us
    pallas_call x1, Pallas kernels, body(): pl.pallas_call(amplitude_kernel, grid=(groups,), in_specs=[pl.BlockSpec((...  3.66 us
    concatenate x1, other arithmetic, body(): jnp.concatenate([first.reshape(row_count * SLOT, lanes), jnp.pad(weights....  2.9 us
  transfers between devices with their start and end apart: 3, of which 2 were waited for; matrix products, arithmetic and copies ran while one was open for 3% of the time, Pallas kernels for 3%

profile of v1, /device:TPU:1, one launch (start us, length us, event | category | flops | bytes accessed | tf_op | source)
XLA Modules:
  0.0 143.0 jit_solution(4772379493985551949)
XLA Ops:
  6.5 0.0 copy-start.3
  6.5 0.0 copy-start.1
  6.5 0.0 all-gather.2.cloned.1.call-start
  6.5 1.2 reshape.26
  7.8 0.0 copy-start.2
  7.8 0.1 pad.17
  7.9 0.0 copy-done.3
  7.9 0.0 copy-done.1
  7.9 2.9 %fusion.6 = bf16[960,256]{1,0:T(8,128)(2,1)} fusion(s32[]{:T(128)S(6)} %select_n.3, bf16[1024,256]{1,0:T(8,128)(2,1)S(1)} %bitcast.18, bf16[96,250]{1,0:T(8,128)(2,1)S(1)} %bitcast.22, bf16[800,250]{1,0:T(8,128)(2,1)S(1)} %bitcast.20), kind=kLoop, calls=%fused_computation.11 | loop fusion | flops 3194880 | bytes 1464832 | tf_op jit(solution)/shard_map/concatenate | solution.py:71
  10.8 0.0 all-gather.2.cloned.1.call-update
  10.8 0.0 copy-done.2
  10.8 0.4 copy.5
  11.2 0.5 reshape.23
  11.7 0.3 copy.7
  12.0 0.9 pad.16.clone
  12.9 0.8 broadcast_in_dim.7
  13.7 0.1 broadcast_in_dim.8
  13.9 50.1 %all_to_all.10 = bf16[16,2,96,128]{3,2,1,0:T(8,128)(2,1)} all-to-all(bf16[16,2,96,128]{3,2,1,0:T(8,128)(2,1)S(1)} %bitcast.17), channel_id=1, replica_groups=mesh['p'=16,'c'=2,'y'=8,'zh'=2] {'y','zh'}, dimensions={0} | all-to-all | bytes 1572864 | tf_op jit(solution)/shard_map/all_to_all | solution.py:83
  64.0 10.5 %all-to-all-start.1 = ((bf16[32,96,128]{2,1,0:T(8,128)(2,1)}), bf16[32,96,128]{2,1,0:T(8,128)(2,1)S(1)}, u32[]{:S(2)}, u32[]{:S(2)}) async-start(bf16[32,96,128]{2,1,0:T(8,128)(2,1)} %bitcast.5), calls=%async_computation.1 | async-start | bytes 1572864 | tf_op jit(solution)/shard_map/all_to_all | solution.py:84
  74.6 0.6 pad_add_fusion.where_ref
  75.2 21.0 %all-to-all-done.1.mirrored_ref = bf16[32,96,128]{2,1,0:T(8,128)(2,1)S(1)} async-done(((bf16[32,96,128]{2,1,0:T(8,128)(2,1)}), bf16[32,96,128]{2,1,0:T(8,128)(2,1)S(1)}, u32[]{:S(2)}, u32[]{:S(2)}) %all-to-all-start.1) | async-done | bytes 786464 | tf_op jit(solution)/shard_map/all_to_all | solution.py:84
  96.2 0.0 copy-start
  96.2 0.9 copy-done
  97.1 3.7 %amplitude.1.amplitude_ref = bf16[384,1024]{1,0:T(8,128)(2,1)} custom-call(bf16[8,4,96,128]{3,2,1,0:T(8,128)(2,1)} %bitcast.4.direct_ref, bf16[32,96,128]{2,1,0:T(8,128)(2,1)} %copy-done), custom_call_target="tpu_custom_call" | custom-call | tf_op jit(solution)/shard_map/amplitude/pallas_call | solution.py:85
  100.7 0.0 all-gather.2.cloned.1.call-done
  100.7 11.7 %contraction.1 = (f32[192,800]{1,0:T(8,128)}, bf16[192,800]{1,0:T(8,128)(2,1)}) custom-call(s32[2]{0:T(128)} %pad_add_fusion.where_ref, bf16[384,1024]{1,0:T(8,128)(2,1)} %amplitude.1.amplitude_ref, bf16[8,1920,256]{2,1,0:T(8,128)(2,1)} %bitcast.15), custom_call_target="tpu_custom_call" | custom-call | tf_op jit(solution)/shard_map/contraction/pallas_call | solution.py:99
  112.4 1.9 %collective-permute-start = (bf16[192,800]{1,0:T(8,128)(2,1)}, bf16[192,800]{1,0:T(8,128)(2,1)S(1)}, u32[]{:S(2)}, u32[]{:S(2)}) collective-permute-start(bf16[192,800]{1,0:T(8,128)(2,1)} %get-tuple-element.8), channel_id=1, source_target_pairs={{0,1},{1,0},{2,3},{3,2},{4,5},{5,4},{6,7},{7,6},{8,9},{9,8},{10,11... | collective-permute-start | bytes 921608 | tf_op jit(solution)/shard_map/ppermute | solution.py:115
  114.3 20.0 %collective-permute-done = bf16[192,800]{1,0:T(8,128)(2,1)S(1)} collective-permute-done((bf16[192,800]{1,0:T(8,128)(2,1)}, bf16[192,800]{1,0:T(8,128)(2,1)S(1)}, u32[]{:S(2)}, u32[]{:S(2)}) %collective-permute-start) | collective-permute-done | bytes 307232 | tf_op jit(solution)/shard_map/ppermute | solution.py:115
  134.3 1.9 %add_convert_fusion = bf16[192,800]{1,0:T(8,128)(2,1)} fusion(f32[192,800]{1,0:T(8,128)} %get-tuple-element.7, bf16[192,800]{1,0:T(8,128)(2,1)S(1)} %collective-permute-done), kind=kLoop, calls=%fused_computation.10 | loop fusion | flops 460800 | bytes 1228800 | tf_op jit(solution)/shard_map/convert_element_type | solution.py:116
Async XLA Ops:
  6.5 1.4 copy-start.3
  6.5 1.4 copy-start.1
  6.5 94.2 %all-gather.2.cloned.1.call-start = ((), (), s32[]{:S(2)}) async-start(), calls=%async_computation.2 | async-start | bytes 8355840 | tf_op jit(solution)/shard_map/all_gather | solution.py:76
  7.8 3.1 %copy-start.2 = (bf16[96,25,50]{0,2,1:T(8,128)(2,1)S(1)}, bf16[96,25,50]{0,2,1:T(8,128)(2,1)}, u32[]{:S(2)}) copy-start(bf16[96,25,50]{0,2,1:T(8,128)(2,1)} %param.4) | copy-start | bytes 720004
  64.0 32.1 %all-to-all-start.1 = ((bf16[32,96,128]{2,1,0:T(8,128)(2,1)}), bf16[32,96,128]{2,1,0:T(8,128)(2,1)S(1)}, u32[]{:S(2)}, u32[]{:S(2)}) async-start(bf16[32,96,128]{2,1,0:T(8,128)(2,1)} %bitcast.5), calls=%async_computation.1 | async-start | bytes 1572864 | tf_op jit(solution)/shard_map/all_to_all | solution.py:84
  96.2 0.9 copy-start
  112.4 21.9 %collective-permute-start = (bf16[192,800]{1,0:T(8,128)(2,1)}, bf16[192,800]{1,0:T(8,128)(2,1)S(1)}, u32[]{:S(2)}, u32[]{:S(2)}) collective-permute-start(bf16[192,800]{1,0:T(8,128)(2,1)} %get-tuple-element.8), channel_id=1, source_target_pairs={{0,1},{1,0},{2,3},{3,2},{4,5},{5,4},{6,7},{7,6},{8,9},{9,8},{10,11... | collective-permute-start | bytes 921608 | tf_op jit(solution)/shard_map/ppermute | solution.py:115
Sparse Core Ops, SparseCore 0:
  11.0 78.4 all-gather.1

commit v2 on v0

v2 whole, which is shorter than its diff:
```python
import functools

import jax
import jax.numpy as jnp
from jax import lax
from jax.experimental import pallas as pl
from jax.experimental.pallas import tpu as pltpu
from jax.sharding import Mesh, PartitionSpec as P

ROWS, SLOT, LANES = 25, 32, 128
F32, BF16 = jnp.float32, jnp.bfloat16


def pack_kernel(core_ref, first_hbm, weights_hbm, second_hbm, out_ref, held, sems):
    virtual, block = first_hbm.shape
    half = weights_hbm.shape[0] // 2
    out_ref[:, LANES:] = jnp.zeros((out_ref.shape[0], out_ref.shape[1] - LANES), BF16)

    @pl.when(core_ref[0] == 0)
    def _():
        big = pltpu.make_async_copy(first_hbm, held.at[pl.ds(0, virtual)], sems.at[0])
        small = pltpu.make_async_copy(weights_hbm.at[pl.ds(0, half)], held.at[pl.ds(virtual, half)], sems.at[1])
        big.start()
        small.start()
        big.wait()
        small.wait()

    @pl.when(core_ref[0] != 0)
    def _():
        small = pltpu.make_async_copy(weights_hbm.at[pl.ds(half, half)], held.at[pl.ds(0, half)], sems.at[1])
        big = pltpu.make_async_copy(second_hbm, held.at[pl.ds(half, virtual)], sems.at[0])
        big.start()
        small.start()
        big.wait()
        small.wait()

    out_ref[:, :block] = held[...]


def direct_kernel(pieces_ref, out_ref, wide_ref, pick_ref):
    count = pieces_ref.shape[0]
    groups = out_ref.shape[0] // LANES
    depth, width = pick_ref.shape
    at = lax.broadcasted_iota(jnp.int32, (depth, width), 0)
    to = lax.broadcasted_iota(jnp.int32, (depth, width), 1)
    within = at % SLOT
    target = jnp.where(within < ROWS, (at // SLOT) * ROWS + within, -1)
    pick_ref[...] = jnp.where(target == to, 1.0, 0.0).astype(BF16)
    lane = lax.broadcasted_iota(jnp.int32, (ROWS, LANES), 1) // SLOT
    wide_ref[...] = jnp.zeros_like(wide_ref)
    for quad in range(count // 4):
        whole = [pieces_ref[4 * quad + k].astype(F32) for k in range(4)]
        for group in range(groups):
            parts = [w[group * ROWS : (group + 1) * ROWS] for w in whole]
            for orbital in range(4):
                placed = None
                for k in range(4):
                    shift = SLOT * ((k - orbital) % 4)
                    moved = pltpu.roll(parts[k], shift, 1) if shift else parts[k]
                    placed = moved if placed is None else jnp.where(lane == k, moved, placed)
                row = (4 * group + orbital) * SLOT
                wide_ref[row : row + ROWS, quad * LANES : (quad + 1) * LANES] = placed
    out_ref[...] = jnp.dot(wide_ref[...].astype(BF16), pick_ref[...], preferred_element_type=F32).astype(BF16)


def amplitude_kernel(direct_ref, pieces_ref, out_ref, flat_ref):
    count = pieces_ref.shape[0]
    groups = out_ref.shape[0] // LANES
    for source in range(count):
        whole = pieces_ref[source].astype(F32)
        for group in range(groups):
            flat_ref[group, source * ROWS : (source + 1) * ROWS, :] = whole[group * ROWS : (group + 1) * ROWS]
    for group in range(groups):
        rows = slice(group * LANES, (group + 1) * LANES)
        mirrored = jnp.transpose(flat_ref[group])
        out_ref[rows, :] = (direct_ref[rows, :].astype(F32) - mirrored).astype(BF16)


def contraction_kernel(where_ref, amplitude_ref, factors_hbm, own_ref, other_ref, held, total_ref, sems, *, orbitals):
    rows, depth = amplitude_ref.shape
    chunks = sems.shape[0]
    per = factors_hbm.shape[0] // chunks
    copies = [
        pltpu.make_async_copy(factors_hbm.at[pl.ds(j * per, per)], held.at[pl.ds(j * per, per)], sems.at[j])
        for j in range(chunks)
    ]
    for copy in copies:
        copy.start()
    pick = lax.broadcasted_iota(jnp.int32, (rows, orbitals), 0) // SLOT + where_ref[0]
    pick = (pick == lax.broadcasted_iota(jnp.int32, (rows, orbitals), 1)).astype(BF16)
    amplitude = amplitude_ref[...]
    total = None
    for j in range(chunks):
        copies[j].wait()
        scaled, second = [], []
        for k in range(j * per, (j + 1) * per):
            value = jnp.dot(amplitude, held[k, :depth], preferred_element_type=F32)
            scale = jnp.dot(pick, held[k, depth : depth + orbitals], preferred_element_type=F32)
            scaled.append((value * scale).astype(BF16))
            second.append(held[k, depth + orbitals :])
        part = lax.dot_general(
            jnp.concatenate(scaled, 1), jnp.concatenate(second, 1), (((1,), (1,)), ((), ())), preferred_element_type=F32
        )
        total = part if total is None else total + part
    total_ref[...] = total
    half = rows // 2
    mine = where_ref[1]
    own_ref[...] = total_ref[pl.ds(pl.multiple_of(mine * half, half), half), :]
    other = total_ref[pl.ds(pl.multiple_of((1 - mine) * half, half), half), :]
    other = [other[k * SLOT : k * SLOT + ROWS] for k in range(half // SLOT)]
    other_ref[...] = jnp.concatenate(other, 0).astype(BF16)


def finish_kernel(own_ref, received_ref, out_ref):
    received = received_ref[...].astype(F32)
    for k in range(out_ref.shape[0]):
        out_ref[k] = (own_ref[k * SLOT : k * SLOT + ROWS] + received[k * ROWS : (k + 1) * ROWS]).astype(BF16)


def vmem(count):
    return [pl.BlockSpec(memory_space=pltpu.VMEM)] * count


def hbm(count):
    return [pl.BlockSpec(memory_space=pl.ANY)] * count


SMEM = [pl.BlockSpec(memory_space=pltpu.SMEM)]
ROOM = pltpu.CompilerParams(vmem_limit_bytes=32 * 2**20)
SMALL = pltpu.CompilerParams(vmem_limit_bytes=16 * 2**20)


def body(halves, first_factor, second_factor, weights):
    y_count, row_count = lax.axis_size("y"), lax.axis_size("p") * 2
    orbitals = halves.shape[0]
    block, virtual = first_factor.shape
    local = orbitals // y_count
    groups = local // 4
    y, zh, core = lax.axis_index("y"), lax.axis_index("zh"), lax.axis_index("c")

    lanes = (block + LANES - 1) // LANES * LANES
    half = virtual + orbitals // 2
    share = pl.pallas_call(
        pack_kernel,
        in_specs=SMEM + hbm(3),
        out_specs=vmem(1)[0],
        out_shape=jax.ShapeDtypeStruct((half, lanes), BF16),
        scratch_shapes=[pltpu.VMEM((half, block), BF16), pltpu.SemaphoreType.DMA((2,))],
        compiler_params=SMALL,
        name="pack",
    )(core.reshape(1), first_factor.T, weights.T, second_factor.T)
    factors = lax.all_gather(share, ("y", "c"), axis=0, tiled=True).reshape(y_count, 2 * half, lanes)

    used = groups * ROWS
    piece = (used + 15) // 16 * 16
    pieces = halves.reshape(y_count, groups, 4, ROWS, 2, ROWS).transpose(0, 4, 1, 3, 2, 5)
    pieces = jnp.pad(pieces, ((0, 0),) * 5 + ((0, SLOT - ROWS),)).reshape(y_count, 1, 2, used, LANES)
    pieces = jnp.pad(pieces, ((0, 0),) * 3 + ((0, piece - used), (0, 0)))
    pieces = jnp.broadcast_to(pieces, (y_count, 2, 2, piece, LANES)).reshape(2 * y_count, 2, piece, LANES)
    direct = lax.all_to_all(pieces, ("y", "zh"), 0, 0, tiled=True).reshape(row_count, piece, LANES)
    mirrored = lax.all_to_all(direct, ("p", "c"), 0, 0, tiled=True)
    rows = local * SLOT
    laid = jax.ShapeDtypeStruct((rows, virtual), BF16)
    direct = pl.pallas_call(
        direct_kernel,
        in_specs=vmem(1),
        out_specs=vmem(1)[0],
        out_shape=laid,
        scratch_shapes=[pltpu.VMEM((rows, row_count * SLOT), F32), pltpu.VMEM((row_count * SLOT, virtual), BF16)],
        compiler_params=ROOM,
        cost_estimate=pl.CostEstimate(flops=2 * rows * row_count * SLOT * virtual, bytes_accessed=4 * rows * virtual, transcendentals=0),
        name="direct",
    )(direct)
    amplitude = pl.pallas_call(
        amplitude_kernel,
        in_specs=vmem(2),
        out_specs=vmem(1)[0],
        out_shape=laid,
        scratch_shapes=[pltpu.VMEM((groups, virtual, LANES), F32)],
        compiler_params=ROOM,
        name="amplitude",
    )(direct, mirrored)

    kept = rows // 2
    sent = local // 2 * ROWS
    chunks = max(y_count // 2, 1)
    own, other = pl.pallas_call(
        functools.partial(contraction_kernel, orbitals=orbitals),
        in_specs=SMEM + vmem(1) + hbm(1),
        out_specs=vmem(2),
        out_shape=[jax.ShapeDtypeStruct((kept, virtual), F32), jax.ShapeDtypeStruct((sent, virtual), BF16)],
        scratch_shapes=[
            pltpu.VMEM((y_count, 2 * half, lanes), BF16),
            pltpu.VMEM((rows, virtual), F32),
            pltpu.SemaphoreType.DMA((chunks,)),
        ],
        compiler_params=ROOM,
        name="contraction",
    )(jnp.stack([y * local, zh]), amplitude, factors)
    received = lax.ppermute(other, "zh", [(0, 1), (1, 0)])
    return pl.pallas_call(
        finish_kernel,
        in_specs=vmem(2),
        out_specs=vmem(1)[0],
        out_shape=jax.ShapeDtypeStruct((local // 2, ROWS, virtual), BF16),
        compiler_params=SMALL,
        name="finish",
    )(own, received)


def solution(mesh):
    rows, columns = mesh.devices.shape
    fine = Mesh(mesh.devices.reshape(rows // 2, 2, columns // 2, 2), ("p", "c", "y", "zh"))
    row, col = ("p", "c"), ("y", "zh")
    placed = (P(None, row, col), P(col, None), P(col, None), P(col, None))
    return jax.shard_map(body, mesh=fine, in_specs=placed, out_specs=P(col, row, None), check_vma=False)
```

time: 385 us -> 126 us (0.33)
  waiting for transfers between devices: 194 us -> 33.2 us
  blocking collectives: 98 us -> 45.9 us
  local copies, waits for them, and re-layouts: 47.3 us -> 8.32 us
  matrix products: 12.3 us -> 0 us
  Pallas kernels: 0 us -> 11.4 us
  other arithmetic: 4.32 us -> 0.08 us
    all_gather x2 -> x1, waiting for transfers between devices: 193 us -> 0.02 us  [body(): lax.all_gather(share, ('y', 'c'), axis=0, tiled=True)]
    all_gather x1 -> x0, blocking collectives: 67.8 us -> none  [body(): scale_piece = lax.all_gather(weights, 'col', axis=0, tiled=True)]
    unnamed x11 -> x12, local copies, waits for them, and re-layouts: 25.5 us -> 6.45 us
    ppermute x0 -> x1, waiting for transfers between devices: none -> 17 us  [body(): received = lax.ppermute(other, 'zh', [(0, 1), (1, 0)])]
    all_to_all x1, waiting for transfers between devices: 0.01 us -> 16.2 us  [body(): mirrored = lax.all_to_all(direct, ('p', 'c'), 0, 0, tiled=True)]
    all_to_all x1, blocking collectives: 30.2 us -> 45.9 us  [body(): lax.all_to_all(pieces, ('y', 'zh'), 0, 0, tiled=True)]
    dot_general x2 -> x0, matrix products: 12.3 us -> none  [the longest x1 7.65 us: body(): jnp.einsum('iakq,kqc->kiac', scaled, second_piece.reshape(block_count, bl...]
    pallas_call x0 -> x5, Pallas kernels: none -> 11.4 us  [the longest x1 6.36 us: body(): pl.pallas_call(functools.partial(contraction_kernel, orbitals=orbitals),...]
  transfers between devices with their start and end apart: 3 -> 3, of which waited for: 2 -> 2; matrix products, arithmetic and copies ran while one was open for 13% -> 2% of each run, Pallas kernels for 0% -> 2%
where the time goes in v2:
time: 126 us; the launch traced here: 125 us
  blocking collectives  45.9 us (36%)
  waiting for transfers between devices  33.2 us (26%)
  between operations  13.5 us (11%)
  starting transfers between devices  12.7 us (10%)
  Pallas kernels  11.4 us (9%)
  local copies, waits for them, and re-layouts  8.32 us (7%)
    all_to_all x1, blocking collectives, body(): lax.all_to_all(pieces, ('y', 'zh'), 0, 0, tiled=True)  45.9 us
    ppermute x1, waiting for transfers between devices, body(): received = lax.ppermute(other, 'zh', [(0, 1), (1, 0)])  17 us
    all_to_all x1, waiting for transfers between devices, body(): mirrored = lax.all_to_all(direct, ('p', 'c'), 0, 0, tiled=True)  16.2 us
    all_to_all x1, starting transfers between devices, body(): mirrored = lax.all_to_all(direct, ('p', 'c'), 0, 0, tiled=True)  10.8 us
    unnamed x12, local copies, waits for them, and re-layouts  6.45 us
    pallas_call x1, Pallas kernels, body(): pl.pallas_call(functools.partial(contraction_kernel, orbitals=orbitals),...  6.36 us
    pallas_call x1, Pallas kernels, body(): pl.pallas_call(direct_kernel, in_specs=vmem(1), out_specs=vmem(1)[0], out...  2.77 us
  transfers between devices with their start and end apart: 3, of which 2 were waited for; matrix products, arithmetic and copies ran while one was open for 2% of the time, Pallas kernels for 2%

profile of v2, /device:TPU:1, one launch (start us, length us, event | category | flops | bytes accessed | tf_op | source)
XLA Modules:
  0.0 125.1 jit_solution(1557031996299439310)
XLA Ops:
  6.5 0.0 all-gather.2.cloned.1.call-start
  6.5 0.0 copy-start.1
  6.5 1.0 copy-done.1
  7.5 0.0 copy-start.2
  7.5 1.0 copy-done.2
  8.5 0.0 copy-start.3
  8.5 0.8 copy-done.3
  9.3 0.0 copy-start.4
  9.3 1.1 pack.1
  10.4 0.0 all-gather.2.cloned.1.call-update
  10.5 0.0 copy-done.4
  10.5 0.4 copy.5
  10.8 0.5 reshape.18
  11.3 0.3 copy.8
  11.6 0.6 pad.8.clone
  12.3 0.6 reshape.19
  13.0 0.1 broadcast_in_dim.8
  13.1 45.9 %all_to_all.10 = bf16[16,2,80,128]{3,2,1,0:T(8,128)(2,1)} all-to-all(bf16[16,2,80,128]{3,2,1,0:T(8,128)(2,1)S(1)} %bitcast.21), channel_id=1, replica_groups=mesh['p'=16,'c'=2,'y'=8,'zh'=2] {'y','zh'}, dimensions={0} | all-to-all | bytes 1310720 | tf_op jit(solution)/shard_map/all_to_all | solution.py:160
  58.9 10.8 %all-to-all-start.1 = ((bf16[32,80,128]{2,1,0:T(8,128)(2,1)}), bf16[32,80,128]{2,1,0:T(8,128)(2,1)S(1)}, u32[]{:S(2)}, u32[]{:S(2)}) async-start(bf16[32,80,128]{2,1,0:T(8,128)(2,1)} %bitcast.5.pieces_ref), calls=%async_computation.1 | async-start | bytes 1310720 | tf_op jit(solution)/shard_map/all_to_all | solution.py:161
  69.7 0.1 pad_add_fusion.where_ref
  69.8 2.8 %direct.1.direct_ref = bf16[384,800]{1,0:T(8,128)(2,1)S(1)} custom-call(bf16[32,80,128]{2,1,0:T(8,128)(2,1)} %bitcast.5.pieces_ref), custom_call_target="tpu_custom_call" | custom-call | flops 629145600 | bytes 1228800 | tf_op jit(solution)/shard_map/direct/pallas_call | solution.py:164
  72.6 16.2 %all-to-all-done.1.pieces_ref = bf16[32,80,128]{2,1,0:T(8,128)(2,1)S(1)} async-done(((bf16[32,80,128]{2,1,0:T(8,128)(2,1)}), bf16[32,80,128]{2,1,0:T(8,128)(2,1)S(1)}, u32[]{:S(2)}, u32[]{:S(2)}) %all-to-all-start.1) | async-done | bytes 655392 | tf_op jit(solution)/shard_map/all_to_all | solution.py:161
  88.8 0.4 amplitude.1.amplitude_ref
  89.1 0.0 all-gather.2.cloned.1.call-done
  89.1 0.0 copy-start
  89.2 3.0 %copy-done = bf16[13568,256]{1,0:T(8,128)(2,1)S(1)} copy-done((bf16[13568,256]{1,0:T(8,128)(2,1)S(1)}, bf16[13568,256]{1,0:T(8,128)(2,1)}, u32[]{:S(2)}) %copy-start) | copy-done | bytes 6946840
  92.1 6.4 %contraction.1 = (f32[192,800]{1,0:T(8,128)S(1)}, bf16[150,800]{1,0:T(8,128)(2,1)S(1)}) custom-call(s32[2]{0:T(128)S(1)} %pad_add_fusion.where_ref, bf16[384,800]{1,0:T(8,128)(2,1)S(1)} %amplitude.1.amplitude_ref, bf16[8,1696,256]{2,1,0:T(8,128)(2,1)S(1)} %bitcast.16), custom_call_target="tpu_custom_call" | custom-call | tf_op jit(solution)/shard_map/contraction/pallas_call | solution.py:187
  98.5 1.9 %collective-permute-start = (bf16[150,800]{1,0:T(8,128)(2,1)S(1)}, bf16[150,800]{1,0:T(8,128)(2,1)S(1)}, u32[]{:S(2)}, u32[]{:S(2)}) collective-permute-start(bf16[150,800]{1,0:T(8,128)(2,1)S(1)} %get-tuple-element.8), channel_id=1, source_target_pairs={{0,1},{1,0},{2,3},{3,2},{4,5},{5,4},{6,7},{7,6},{8,9},{9,8},{10,11... | collective-permute-start | bytes 720008 | tf_op jit(solution)/shard_map/ppermute | solution.py:200
  100.4 17.0 %collective-permute-done.received_ref = bf16[150,800]{1,0:T(8,128)(2,1)S(1)} collective-permute-done((bf16[150,800]{1,0:T(8,128)(2,1)S(1)}, bf16[150,800]{1,0:T(8,128)(2,1)S(1)}, u32[]{:S(2)}, u32[]{:S(2)}) %collective-permute-start) | collective-permute-done | bytes 240032 | tf_op jit(solution)/shard_map/ppermute | solution.py:200
  117.5 0.8 finish.1
  (2 shorter events, 0.1 us)
Async XLA Ops:
  6.5 82.6 %all-gather.2.cloned.1.call-start = ((), (), s32[]{:S(2)}) async-start(), calls=%async_computation.2 | async-start | bytes 7380992 | tf_op jit(solution)/shard_map/all_gather | solution.py:152
  6.5 1.0 copy-start.1
  7.5 1.0 copy-start.2
  8.5 0.8 copy-start.3
  9.3 1.1 copy-start.4
  58.9 29.8 %all-to-all-start.1 = ((bf16[32,80,128]{2,1,0:T(8,128)(2,1)}), bf16[32,80,128]{2,1,0:T(8,128)(2,1)S(1)}, u32[]{:S(2)}, u32[]{:S(2)}) async-start(bf16[32,80,128]{2,1,0:T(8,128)(2,1)} %bitcast.5.pieces_ref), calls=%async_computation.1 | async-start | bytes 1310720 | tf_op jit(solution)/shard_map/all_to_all | solution.py:161
  89.1 3.0 %copy-start = (bf16[13568,256]{1,0:T(8,128)(2,1)S(1)}, bf16[13568,256]{1,0:T(8,128)(2,1)}, u32[]{:S(2)}) copy-start(bf16[13568,256]{1,0:T(8,128)(2,1)} %all-gather.2.cloned.1.call-done) | copy-start | bytes 20840452
  98.5 19.0 %collective-permute-start = (bf16[150,800]{1,0:T(8,128)(2,1)S(1)}, bf16[150,800]{1,0:T(8,128)(2,1)S(1)}, u32[]{:S(2)}, u32[]{:S(2)}) collective-permute-start(bf16[150,800]{1,0:T(8,128)(2,1)S(1)} %get-tuple-element.8), channel_id=1, source_target_pairs={{0,1},{1,0},{2,3},{3,2},{4,5},{5,4},{6,7},{7,6},{8,9},{9,8},{10,11... | collective-permute-start | bytes 720008 | tf_op jit(solution)/shard_map/ppermute | solution.py:200
Sparse Core Ops, SparseCore 0:
  10.6 70.8 all-gather.1

commit v3 on v2

v3 whole, which is shorter than its diff:
```python
import functools

import jax
import jax.numpy as jnp
from jax import lax
from jax.experimental import pallas as pl
from jax.experimental.pallas import tpu as pltpu
from jax.sharding import Mesh, PartitionSpec as P

ROWS, SLOT, LANES = 25, 32, 128
F32, BF16 = jnp.float32, jnp.bfloat16


def pack_kernel(part_ref, first_hbm, weights_hbm, second_hbm, out_ref, held, sems):
    virtual, block = first_hbm.shape
    orbitals = weights_hbm.shape[0]
    rows = out_ref.shape[0]
    used = 2 * virtual + orbitals
    sources = ((first_hbm, 0, virtual), (weights_hbm, virtual, orbitals), (second_hbm, virtual + orbitals, virtual))
    copies = [
        pltpu.make_async_copy(ref, held.at[pl.ds(start, size)], sems.at[j]) for j, (ref, start, size) in enumerate(sources)
    ]
    for copy in copies:
        copy.start()
    if held.shape[0] > used:
        held[used:, :] = jnp.zeros((held.shape[0] - used, block), BF16)
    out_ref[:, LANES:] = jnp.zeros((rows, out_ref.shape[1] - LANES), BF16)
    for copy in copies:
        copy.wait()
    out_ref[:, :block] = held[pl.ds(pl.multiple_of(part_ref[0] * rows, rows), rows), :]


def direct_kernel(pieces_ref, out_ref, wide_ref, pick_ref):
    count = pieces_ref.shape[0]
    orbitals = out_ref.shape[0] // SLOT
    groups = -(-orbitals // 4)
    depth, width = pick_ref.shape
    at = lax.broadcasted_iota(jnp.int32, (depth, width), 0)
    to = lax.broadcasted_iota(jnp.int32, (depth, width), 1)
    within = at % SLOT
    target = jnp.where(within < ROWS, (at // SLOT) * ROWS + within, -1)
    pick_ref[...] = jnp.where(target == to, 1.0, 0.0).astype(BF16)
    lane = lax.broadcasted_iota(jnp.int32, (ROWS, LANES), 1) // SLOT
    wide_ref[...] = jnp.zeros_like(wide_ref)
    for quad in range(count // 4):
        whole = [pieces_ref[4 * quad + k].astype(F32) for k in range(4)]
        for group in range(groups):
            parts = [w[group * ROWS : (group + 1) * ROWS] for w in whole]
            for orbital in range(min(4, orbitals - 4 * group)):
                placed = None
                for k in range(4):
                    shift = SLOT * ((k - orbital) % 4)
                    moved = pltpu.roll(parts[k], shift, 1) if shift else parts[k]
                    placed = moved if placed is None else jnp.where(lane == k, moved, placed)
                row = (4 * group + orbital) * SLOT
                wide_ref[row : row + ROWS, quad * LANES : (quad + 1) * LANES] = placed
    out_ref[...] = jnp.dot(wide_ref[...].astype(BF16), pick_ref[...], preferred_element_type=F32).astype(BF16)


def amplitude_kernel(direct_ref, pieces_ref, out_ref, flat_ref):
    count = pieces_ref.shape[0]
    orbitals = out_ref.shape[0] // SLOT
    groups = -(-orbitals // 4)
    for source in range(count):
        whole = pieces_ref[source].astype(F32)
        for group in range(groups):
            flat_ref[group, source * ROWS : (source + 1) * ROWS, :] = whole[group * ROWS : (group + 1) * ROWS]
    for group in range(groups):
        count = min(4, orbitals - 4 * group) * SLOT
        rows = slice(group * LANES, group * LANES + count)
        mirrored = jnp.transpose(flat_ref[group])[:count]
        out_ref[rows, :] = (direct_ref[rows, :].astype(F32) - mirrored).astype(BF16)


def contraction_kernel(where_ref, amplitude_ref, factors_hbm, out_ref, held, sems, *, orbitals):
    rows, depth = amplitude_ref.shape
    chunks = sems.shape[0]
    per = factors_hbm.shape[0] // chunks
    copies = [
        pltpu.make_async_copy(factors_hbm.at[pl.ds(j * per, per)], held.at[pl.ds(j * per, per)], sems.at[j])
        for j in range(chunks)
    ]
    for copy in copies:
        copy.start()
    pick = lax.broadcasted_iota(jnp.int32, (rows, orbitals), 0) // SLOT + where_ref[0]
    pick = (pick == lax.broadcasted_iota(jnp.int32, (rows, orbitals), 1)).astype(BF16)
    amplitude = amplitude_ref[...]
    total = None
    for j in range(chunks):
        copies[j].wait()
        scaled, second = [], []
        for k in range(j * per, (j + 1) * per):
            value = jnp.dot(amplitude, held[k, :depth], preferred_element_type=F32)
            scale = jnp.dot(pick, held[k, depth : depth + orbitals], preferred_element_type=F32)
            scaled.append((value * scale).astype(BF16))
            second.append(held[k, depth + orbitals : 2 * depth + orbitals])
        part = lax.dot_general(
            jnp.concatenate(scaled, 1), jnp.concatenate(second, 1), (((1,), (1,)), ((), ())), preferred_element_type=F32
        )
        total = part if total is None else total + part
    for k in range(out_ref.shape[0]):
        out_ref[k] = total[k * SLOT : k * SLOT + ROWS].astype(BF16)


def vmem(count):
    return [pl.BlockSpec(memory_space=pltpu.VMEM)] * count


def hbm(count):
    return [pl.BlockSpec(memory_space=pl.ANY)] * count


SMEM = [pl.BlockSpec(memory_space=pltpu.SMEM)]
ROOM = pltpu.CompilerParams(vmem_limit_bytes=32 * 2**20)
FULL = pltpu.CompilerParams(vmem_limit_bytes=60 * 2**20)


def body(halves, first_factor, second_factor, weights):
    blocks, row_count = lax.axis_size("y") * lax.axis_size("zh"), lax.axis_size("zl") * lax.axis_size("x") * 2
    orbitals = halves.shape[0]
    block, virtual = first_factor.shape
    local = orbitals // blocks
    groups = -(-local // 4)
    column = lax.axis_index(("y", "zh"))

    lanes = -(-block // LANES) * LANES
    parts = lax.axis_size("zl") * 2
    height = -(-(2 * virtual + orbitals) // (16 * parts)) * 16
    share = pl.pallas_call(
        pack_kernel,
        in_specs=SMEM + hbm(3),
        out_specs=vmem(1)[0],
        out_shape=jax.ShapeDtypeStruct((height, lanes), BF16),
        scratch_shapes=[pltpu.VMEM((parts * height, block), BF16), pltpu.SemaphoreType.DMA((3,))],
        compiler_params=FULL,
        name="pack",
    )(lax.axis_index(("zl", "c")).reshape(1), first_factor.T, weights.T, second_factor.T)
    factors = lax.all_gather(share, ("y", "zh", "zl", "c"), axis=0, tiled=True).reshape(blocks, parts * height, lanes)

    used = groups * ROWS
    piece = -(-used // 16) * 16
    pieces = halves.reshape(blocks, local, ROWS, 2, ROWS)
    pieces = jnp.pad(pieces, ((0, 0), (0, 4 * groups - local), (0, 0), (0, 0), (0, 0)))
    pieces = pieces.reshape(blocks, groups, 4, ROWS, 2, ROWS).transpose(0, 4, 1, 3, 2, 5)
    pieces = jnp.pad(pieces, ((0, 0),) * 5 + ((0, SLOT - ROWS),)).reshape(blocks, 2, used, LANES)
    pieces = jnp.pad(pieces, ((0, 0), (0, 0), (0, piece - used), (0, 0)))
    direct = lax.all_to_all(pieces, ("y", "zh"), 0, 0, tiled=True).reshape(row_count, piece, LANES)
    mirrored = lax.all_to_all(direct, ("zl", "x", "c"), 0, 0, tiled=True)
    rows = local * SLOT
    laid = jax.ShapeDtypeStruct((rows, virtual), BF16)
    direct = pl.pallas_call(
        direct_kernel,
        in_specs=vmem(1),
        out_specs=vmem(1)[0],
        out_shape=laid,
        scratch_shapes=[pltpu.VMEM((rows, row_count * SLOT), F32), pltpu.VMEM((row_count * SLOT, virtual), BF16)],
        compiler_params=ROOM,
        cost_estimate=pl.CostEstimate(flops=2 * rows * row_count * SLOT * virtual, bytes_accessed=4 * rows * virtual, transcendentals=0),
        name="direct",
    )(direct)
    amplitude = pl.pallas_call(
        amplitude_kernel,
        in_specs=vmem(2),
        out_specs=vmem(1)[0],
        out_shape=laid,
        scratch_shapes=[pltpu.VMEM((groups, virtual, LANES), F32)],
        compiler_params=ROOM,
        name="amplitude",
    )(direct, mirrored)

    chunks = blocks // 2
    return pl.pallas_call(
        functools.partial(contraction_kernel, orbitals=orbitals),
        in_specs=SMEM + vmem(1) + hbm(1),
        out_specs=vmem(1)[0],
        out_shape=jax.ShapeDtypeStruct((local, ROWS, virtual), BF16),
        scratch_shapes=[pltpu.VMEM((blocks, parts * height, lanes), BF16), pltpu.SemaphoreType.DMA((chunks,))],
        compiler_params=FULL,
        name="contraction",
    )((column * local).reshape(1), amplitude, factors)


def solution(mesh):
    rows, columns = mesh.devices.shape
    along_x = 4 if rows % 32 == 0 else 2
    shape = (rows // (2 * along_x), along_x, 2, columns // 2, 2)
    fine = Mesh(mesh.devices.reshape(shape), ("zl", "x", "c", "y", "zh"))
    row, col = ("zl", "x", "c"), ("y", "zh")
    placed = (P(None, row, col), P(col, None), P(col, None), P(col, None))
    return jax.shard_map(body, mesh=fine, in_specs=placed, out_specs=P(col, row, None), check_vma=False)
```

time: 126 us -> 136 us (1.079)
  waiting for transfers between devices: 33.2 us -> 55.7 us
  blocking collectives: 45.9 us -> 38.2 us
  starting transfers between devices: 12.7 us -> 9.56 us
  local copies, waits for them, and re-layouts: 8.32 us -> 6.24 us
  Pallas kernels: 11.4 us -> 12.8 us
    all_gather x1, waiting for transfers between devices: 0.02 us -> 41.2 us  [body(): lax.all_gather(share, ('y', 'zh', 'zl', 'c'), axis=0, tiled=True)]
    ppermute x1 -> x0, waiting for transfers between devices: 17 us -> none  [body(): received = lax.ppermute(other, 'zh', [(0, 1), (1, 0)])]
    all_to_all x1, blocking collectives: 45.9 us -> 38.2 us  [body(): lax.all_to_all(pieces, ('y', 'zh'), 0, 0, tiled=True)]
    unnamed x12 -> x6, local copies, waits for them, and re-layouts: 6.45 us -> 3.6 us
    pallas_call x1, Pallas kernels: 6.36 us -> 8.56 us  [body(): pl.pallas_call(functools.partial(contraction_kernel, orbitals=orbitals),...]
    ppermute x1 -> x0, starting transfers between devices: 1.92 us -> none  [body(): received = lax.ppermute(other, 'zh', [(0, 1), (1, 0)])]
    all_to_all x1, waiting for transfers between devices: 16.2 us -> 14.5 us  [body(): mirrored = lax.all_to_all(direct, ('zl', 'x', 'c'), 0, 0, tiled=True)]
  transfers between devices with their start and end apart: 3 -> 2, of which waited for: 2 -> 2; matrix products, arithmetic and copies ran while one was open for 2% -> 4% of each run, Pallas kernels for 2% -> 2%
where the time goes in v3:
time: 136 us
  waiting for transfers between devices  55.7 us (41%)
  blocking collectives  38.2 us (28%)
  between operations  13.5 us (10%)
  Pallas kernels  12.8 us (9%)
  starting transfers between devices  9.56 us (7%)
  local copies, waits for them, and re-layouts  6.24 us (5%)
    all_gather x1, waiting for transfers between devices, body(): lax.all_gather(share, ('y', 'zh', 'zl', 'c'), axis=0, tiled=True)  41.2 us
    all_to_all x1, blocking collectives, body(): lax.all_to_all(pieces, ('y', 'zh'), 0, 0, tiled=True)  38.2 us
    all_to_all x1, waiting for transfers between devices, body(): mirrored = lax.all_to_all(direct, ('zl', 'x', 'c'), 0, 0, tiled=True)  14.5 us
    all_to_all x1, starting transfers between devices, body(): mirrored = lax.all_to_all(direct, ('zl', 'x', 'c'), 0, 0, tiled=True)  9.56 us
    pallas_call x1, Pallas kernels, body(): pl.pallas_call(functools.partial(contraction_kernel, orbitals=orbitals),...  8.56 us
    unnamed x6, local copies, waits for them, and re-layouts  3.6 us
  transfers between devices with their start and end apart: 2, of which 2 were waited for; matrix products, arithmetic and copies ran while one was open for 4% of the time, Pallas kernels for 2%

profile of v3, /device:TPU:1, one launch (start us, length us, event | category | flops | bytes accessed | tf_op | source)
XLA Modules:
  0.0 135.9 jit_solution(3466192597533627348)
XLA Ops:
  6.5 0.0 all-gather.2.cloned.1.call-start
  6.5 1.8 %pack.1 = bf16[224,256]{1,0:T(8,128)(2,1)} custom-call(s32[1]{0:T(128)} %bitcast.4.part_ref, bf16[800,250]{1,0:T(8,128)(2,1)} %bitcast.16, bf16[96,250]{1,0:T(8,128)(2,1)} %bitcast.18, bf16[800,250]{1,0:T(8,128)(2,1)} %bitcast.17), custom_call_target="tpu_custom_call" | custom-call | tf_op jit(solution)/shard_map/pack/pallas_call | solution.py:129
  8.4 0.0 all-gather.2.cloned.1.call-update
  8.4 1.3 copy.10
  9.7 0.5 reshape.22
  10.2 0.2 copy.14
  10.4 0.3 pad.12.clone
  10.7 1.2 copy.15
  11.9 1.0 pad.13.clone
  12.9 0.8 reshape.24
  13.8 0.1 copy.16
  13.9 0.1 pad.14.clone
  14.0 38.2 %all_to_all.10 = bf16[16,2,64,128]{3,2,1,0:T(8,128)(2,1)} all-to-all(bf16[16,2,64,128]{3,2,1,0:T(8,128)(2,1)S(1)} %pad.14.clone), channel_id=1, replica_groups=mesh['zl'=4,'x'=4,'c'=2,'y'=8,'zh'=2] {'y','zh'}, dimensions={0} | all-to-all | bytes 1048576 | tf_op jit(solution)/shard_map/all_to_all | solution.py:147
  52.1 9.6 %all-to-all-start.1 = ((bf16[32,64,128]{2,1,0:T(8,128)(2,1)}), bf16[32,64,128]{2,1,0:T(8,128)(2,1)S(1)}, u32[]{:S(2)}, u32[]{:S(2)}) async-start(bf16[32,64,128]{2,1,0:T(8,128)(2,1)} %bitcast.3.pieces_ref), calls=%async_computation.1 | async-start | bytes 1048576 | tf_op jit(solution)/shard_map/all_to_all | solution.py:148
  61.7 2.2 %direct.1.direct_ref = bf16[192,800]{1,0:T(8,128)(2,1)S(1)} custom-call(bf16[32,64,128]{2,1,0:T(8,128)(2,1)} %bitcast.3.pieces_ref), custom_call_target="tpu_custom_call" | custom-call | flops 314572800 | bytes 614400 | tf_op jit(solution)/shard_map/direct/pallas_call | solution.py:151
  63.9 14.5 %all-to-all-done.1.pieces_ref = bf16[32,64,128]{2,1,0:T(8,128)(2,1)S(1)} async-done(((bf16[32,64,128]{2,1,0:T(8,128)(2,1)}), bf16[32,64,128]{2,1,0:T(8,128)(2,1)S(1)}, u32[]{:S(2)}, u32[]{:S(2)}) %all-to-all-start.1) | async-done | bytes 524320 | tf_op jit(solution)/shard_map/all_to_all | solution.py:148
  78.4 0.2 amplitude.1.amplitude_ref
  78.6 0.0 copy-start
  78.6 0.7 copy-done
  79.3 41.2 %all-gather.2.cloned.1.call-done = bf16[28672,256]{1,0:T(8,128)(2,1)} async-done(((bf16[224,256]{1,0:T(8,128)(2,1)}), bf16[28672,256]{1,0:T(8,128)(2,1)}) %all-gather.2.cloned.1.call-update) | async-done | bytes 14680080 | tf_op jit(solution)/shard_map/all_gather | solution.py:138
  120.5 8.6 %contraction.1 = bf16[6,25,800]{2,1,0:T(8,128)(2,1)} custom-call(s32[1]{0:T(128)} %bitcast.where_ref, bf16[192,800]{1,0:T(8,128)(2,1)} %copy-done, bf16[16,1792,256]{2,1,0:T(8,128)(2,1)} %bitcast.14), custom_call_target="tpu_custom_call" | custom-call | tf_op jit(solution)/shard_map/contraction/pallas_call | solution.py:172
Async XLA Ops:
  6.5 114.0 %all-gather.2.cloned.1.call-start = ((), (), s32[]{:S(2)}) async-start(), calls=%async_computation.2 | async-start | bytes 14794752 | tf_op jit(solution)/shard_map/all_gather | solution.py:138
  52.1 26.2 %all-to-all-start.1 = ((bf16[32,64,128]{2,1,0:T(8,128)(2,1)}), bf16[32,64,128]{2,1,0:T(8,128)(2,1)S(1)}, u32[]{:S(2)}, u32[]{:S(2)}) async-start(bf16[32,64,128]{2,1,0:T(8,128)(2,1)} %bitcast.3.pieces_ref), calls=%async_computation.1 | async-start | bytes 1048576 | tf_op jit(solution)/shard_map/all_to_all | solution.py:148
  78.6 0.7 copy-start
Sparse Core Ops, SparseCore 0:
  10.5 110.0 all-gather.1

commit v4 on v2

--- a/solution.py
+++ b/solution.py
@@ -11,30 +11,23 @@
 F32, BF16 = jnp.float32, jnp.bfloat16
 
 
-def pack_kernel(core_ref, first_hbm, weights_hbm, second_hbm, out_ref, held, sems):
+def pack_kernel(part_ref, first_hbm, weights_hbm, second_hbm, out_ref, held, sems):
     virtual, block = first_hbm.shape
-    half = weights_hbm.shape[0] // 2
-    out_ref[:, LANES:] = jnp.zeros((out_ref.shape[0], out_ref.shape[1] - LANES), BF16)
-
-    @pl.when(core_ref[0] == 0)
-    def _():
-        big = pltpu.make_async_copy(first_hbm, held.at[pl.ds(0, virtual)], sems.at[0])
-        small = pltpu.make_async_copy(weights_hbm.at[pl.ds(0, half)], held.at[pl.ds(virtual, half)], sems.at[1])
-        big.start()
-        small.start()
-        big.wait()
-        small.wait()
-
-    @pl.when(core_ref[0] != 0)
-    def _():
-        small = pltpu.make_async_copy(weights_hbm.at[pl.ds(half, half)], held.at[pl.ds(0, half)], sems.at[1])
-        big = pltpu.make_async_copy(second_hbm, held.at[pl.ds(half, virtual)], sems.at[0])
-        big.start()
-        small.start()
-        big.wait()
-        small.wait()
-
-    out_ref[:, :block] = held[...]
+    orbitals = weights_hbm.shape[0]
+    rows = out_ref.shape[0]
+    used = 2 * virtual + orbitals
+    sources = ((first_hbm, 0, virtual), (weights_hbm, virtual, orbitals), (second_hbm, virtual + orbitals, virtual))
+    copies = [
+        pltpu.make_async_copy(ref, held.at[pl.ds(start, size)], sems.at[j]) for j, (ref, start, size) in enumerate(sources)
+    ]
+    for copy in copies:
+        copy.start()
+    if held.shape[0] > used:
+        held[used:, :] = jnp.zeros((held.shape[0] - used, block), BF16)
+    out_ref[:, LANES:] = jnp.zeros((rows, out_ref.shape[1] - LANES), BF16)
+    for copy in copies:
+        copy.wait()
+    out_ref[:, :block] = held[pl.ds(pl.multiple_of(part_ref[0] * rows, rows), rows), :]
 
 
 def direct_kernel(pieces_ref, out_ref, wide_ref, pick_ref):
@@ -76,8 +69,9 @@
         out_ref[rows, :] = (direct_ref[rows, :].astype(F32) - mirrored).astype(BF16)
 
 
-def contraction_kernel(where_ref, amplitude_ref, factors_hbm, own_ref, other_ref, held, total_ref, sems, *, orbitals):
-    rows, depth = amplitude_ref.shape
+def contraction_kernel(where_ref, amplitude_ref, factors_hbm, out_ref, held, sems, *, orbitals, swapped):
+    depth = amplitude_ref.shape[1]
+    rows = amplitude_ref.shape[0] // 2
     chunks = sems.shape[0]
     per = factors_hbm.shape[0] // chunks
     copies = [
@@ -86,9 +80,11 @@
     ]
     for copy in copies:
         copy.start()
-    pick = lax.broadcasted_iota(jnp.int32, (rows, orbitals), 0) // SLOT + where_ref[0]
+    side = 1 - where_ref[1] if swapped else where_ref[1]
+    start = where_ref[0] + side * (rows // SLOT)
+    pick = lax.broadcasted_iota(jnp.int32, (rows, orbitals), 0) // SLOT + start
     pick = (pick == lax.broadcasted_iota(jnp.int32, (rows, orbitals), 1)).astype(BF16)
-    amplitude = amplitude_ref[...]
+    amplitude = amplitude_ref[pl.ds(pl.multiple_of(side * rows, rows), rows), :]
     total = None
     for j in range(chunks):
         copies[j].wait()
@@ -97,24 +93,20 @@
             value = jnp.dot(amplitude, held[k, :depth], preferred_element_type=F32)
             scale = jnp.dot(pick, held[k, depth : depth + orbitals], preferred_element_type=F32)
             scaled.append((value * scale).astype(BF16))
-            second.append(held[k, depth + orbitals :])
+            second.append(held[k, depth + orbitals : 2 * depth + orbitals])
         part = lax.dot_general(
             jnp.concatenate(scaled, 1), jnp.concatenate(second, 1), (((1,), (1,)), ((), ())), preferred_element_type=F32
         )
         total = part if total is None else total + part
-    total_ref[...] = total
-    half = rows // 2
-    mine = where_ref[1]
-    own_ref[...] = total_ref[pl.ds(pl.multiple_of(mine * half, half), half), :]
-    other = total_ref[pl.ds(pl.multiple_of((1 - mine) * half, half), half), :]
-    other = [other[k * SLOT : k * SLOT + ROWS] for k in range(half // SLOT)]
-    other_ref[...] = jnp.concatenate(other, 0).astype(BF16)
+    kept = [total[k * SLOT : k * SLOT + ROWS] for k in range(rows // SLOT)]
+    out_ref[...] = jnp.concatenate(kept, 0).astype(out_ref.dtype)
 
 
 def finish_kernel(own_ref, received_ref, out_ref):
     received = received_ref[...].astype(F32)
     for k in range(out_ref.shape[0]):
-        out_ref[k] = (own_ref[k * SLOT : k * SLOT + ROWS] + received[k * ROWS : (k + 1) * ROWS]).astype(BF16)
+        rows = slice(k * ROWS, (k + 1) * ROWS)
+        out_ref[k] = (own_ref[rows] + received[rows]).astype(BF16)
 
 
 def vmem(count):
@@ -122,12 +114,14 @@
 
 
 def hbm(count):
-    return [pl.BlockSpec(memory_space=pl.ANY)] * count
+    return [pl.BlockSpec(memory_space=pltpu.HBM)] * count
 
 
 SMEM = [pl.BlockSpec(memory_space=pltpu.SMEM)]
 ROOM = pltpu.CompilerParams(vmem_limit_bytes=32 * 2**20)
 SMALL = pltpu.CompilerParams(vmem_limit_bytes=16 * 2**20)
+BIG = pltpu.CompilerParams(vmem_limit_bytes=48 * 2**20)
+FULL = pltpu.CompilerParams(vmem_limit_bytes=60 * 2**20)
 
 
 def body(halves, first_factor, second_factor, weights):
@@ -139,14 +133,14 @@
     y, zh, core = lax.axis_index("y"), lax.axis_index("zh"), lax.axis_index("c")
 
     lanes = (block + LANES - 1) // LANES * LANES
-    half = virtual + orbitals // 2
+    half = (virtual + orbitals // 2 + 15) // 16 * 16
     share = pl.pallas_call(
         pack_kernel,
         in_specs=SMEM + hbm(3),
         out_specs=vmem(1)[0],
         out_shape=jax.ShapeDtypeStruct((half, lanes), BF16),
-        scratch_shapes=[pltpu.VMEM((half, block), BF16), pltpu.SemaphoreType.DMA((2,))],
-        compiler_params=SMALL,
+        scratch_shapes=[pltpu.VMEM((2 * half, block), BF16), pltpu.SemaphoreType.DMA((3,))],
+        compiler_params=FULL,
         name="pack",
     )(core.reshape(1), first_factor.T, weights.T, second_factor.T)
     factors = lax.all_gather(share, ("y", "c"), axis=0, tiled=True).reshape(y_count, 2 * half, lanes)
@@ -181,23 +175,23 @@
         name="amplitude",
     )(direct, mirrored)
 
-    kept = rows // 2
-    sent = local // 2 * ROWS
+    kept = local // 2 * ROWS
     chunks = max(y_count // 2, 1)
-    own, other = pl.pallas_call(
-        functools.partial(contraction_kernel, orbitals=orbitals),
-        in_specs=SMEM + vmem(1) + hbm(1),
-        out_specs=vmem(2),
-        out_shape=[jax.ShapeDtypeStruct((kept, virtual), F32), jax.ShapeDtypeStruct((sent, virtual), BF16)],
-        scratch_shapes=[
-            pltpu.VMEM((y_count, 2 * half, lanes), BF16),
-            pltpu.VMEM((rows, virtual), F32),
-            pltpu.SemaphoreType.DMA((chunks,)),
-        ],
-        compiler_params=ROOM,
-        name="contraction",
-    )(jnp.stack([y * local, zh]), amplitude, factors)
-    received = lax.ppermute(other, "zh", [(0, 1), (1, 0)])
+    where = jnp.stack([y * local, zh])
+
+    def contraction(swapped, dtype):
+        return pl.pallas_call(
+            functools.partial(contraction_kernel, orbitals=orbitals, swapped=swapped),
+            in_specs=SMEM + vmem(1) + hbm(1),
+            out_specs=vmem(1)[0],
+            out_shape=jax.ShapeDtypeStruct((kept, virtual), dtype),
+            scratch_shapes=[pltpu.VMEM((y_count, 2 * half, lanes), BF16), pltpu.SemaphoreType.DMA((chunks,))],
+            compiler_params=BIG,
+            cost_estimate=pl.CostEstimate(flops=kept * virtual * block * y_count * 4, bytes_accessed=y_count * 4 * half * lanes, transcendentals=0),
+            name="contraction_sent" if swapped else "contraction_kept",
+        )(where, amplitude, factors)
+
+    received = lax.ppermute(contraction(True, BF16), "zh", [(0, 1), (1, 0)])
     return pl.pallas_call(
         finish_kernel,
         in_specs=vmem(2),
@@ -205,7 +199,7 @@
         out_shape=jax.ShapeDtypeStruct((local // 2, ROWS, virtual), BF16),
         compiler_params=SMALL,
         name="finish",
-    )(own, received)
+    )(contraction(False, F32), received)
 
 
 def solution(mesh):

time: 126 us -> 119 us (0.944)
  local copies, waits for them, and re-layouts: 8.32 us -> 2.56 us
  waiting for transfers between devices: 33.2 us -> 28.5 us
  Pallas kernels: 11.4 us -> 15.6 us
    unnamed x12 -> x4, local copies, waits for them, and re-layouts: 6.45 us -> 0.69 us
    ppermute x1, waiting for transfers between devices: 17 us -> 12.3 us  [body(): received = lax.ppermute(contraction(True, BF16), 'zh', [(0, 1), (1, 0)])]
    pallas_call x1 -> x2, Pallas kernels: 6.36 us -> 9.57 us  [contraction(): pl.pallas_call(functools.partial(contraction_kernel, orbitals=orbitals, s...]
  transfers between devices with their start and end apart: 3 -> 3, of which waited for: 2 -> 2; matrix products, arithmetic and copies ran while one was open for 2% -> 2% of each run, Pallas kernels for 2% -> 7%
where the time goes in v4:
time: 119 us
  blocking collectives  45.2 us (38%)
  waiting for transfers between devices  28.5 us (24%)
  Pallas kernels  15.6 us (13%)
  between operations  13.5 us (11%)
  starting transfers between devices  13.4 us (11%)
  local copies, waits for them, and re-layouts  2.56 us (2%)
    all_to_all x1, blocking collectives, body(): lax.all_to_all(pieces, ('y', 'zh'), 0, 0, tiled=True)  45.2 us
    all_to_all x1, waiting for transfers between devices, body(): mirrored = lax.all_to_all(direct, ('p', 'c'), 0, 0, tiled=True)  16.2 us
    ppermute x1, waiting for transfers between devices, body(): received = lax.ppermute(contraction(True, BF16), 'zh', [(0, 1), (1, 0)])  12.3 us
    all_to_all x1, starting transfers between devices, body(): mirrored = lax.all_to_all(direct, ('p', 'c'), 0, 0, tiled=True)  11.5 us
    pallas_call x2, Pallas kernels, contraction(): pl.pallas_call(functools.partial(contraction_kernel, orbitals=orbitals, s...  9.57 us
    pallas_call x1, Pallas kernels, body(): pl.pallas_call(direct_kernel, in_specs=vmem(1), out_specs=vmem(1)[0], out...  2.77 us
  transfers between devices with their start and end apart: 3, of which 2 were waited for; matrix products, arithmetic and copies ran while one was open for 2% of the time, Pallas kernels for 7%

profile of v4, /device:TPU:1, one launch (start us, length us, event | category | flops | bytes accessed | tf_op | source)
XLA Modules:
  0.0 118.7 jit_solution(6802517450979559342)
XLA Ops:
  6.5 0.0 copy-start
  6.5 0.0 all-gather.2.cloned.1.call-start
  6.5 2.0 %pack.1 = bf16[848,256]{1,0:T(8,128)(2,1)} custom-call(s32[1]{0:T(128)} %bitcast.6.part_ref, bf16[800,250]{1,0:T(8,128)(2,1)} %bitcast.20, bf16[96,250]{1,0:T(8,128)(2,1)} %bitcast.22, bf16[800,250]{1,0:T(8,128)(2,1)} %bitcast.21), custom_call_target="tpu_custom_call" | custom-call | tf_op jit(solution)/shard_map/pack/pallas_call | solution.py:137
  8.6 0.0 all-gather.2.cloned.1.call-update
  8.6 0.0 copy-done
  8.6 0.4 copy.5
  9.0 0.5 reshape.18
  9.4 0.3 copy.8
  9.8 0.6 pad.8.clone
  10.4 0.6 reshape.19
  11.1 0.1 broadcast_in_dim.8
  11.2 45.2 %all_to_all.10 = bf16[16,2,80,128]{3,2,1,0:T(8,128)(2,1)} all-to-all(bf16[16,2,80,128]{3,2,1,0:T(8,128)(2,1)S(1)} %bitcast.19), channel_id=1, replica_groups=mesh['p'=16,'c'=2,'y'=8,'zh'=2] {'y','zh'}, dimensions={0} | all-to-all | bytes 1310720 | tf_op jit(solution)/shard_map/all_to_all | solution.py:154
  56.4 11.5 %all-to-all-start.1 = ((bf16[32,80,128]{2,1,0:T(8,128)(2,1)}), bf16[32,80,128]{2,1,0:T(8,128)(2,1)S(1)}, u32[]{:S(2)}, u32[]{:S(2)}) async-start(bf16[32,80,128]{2,1,0:T(8,128)(2,1)} %bitcast.5.pieces_ref), calls=%async_computation.1 | async-start | bytes 1310720 | tf_op jit(solution)/shard_map/all_to_all | solution.py:155
  67.9 0.1 pad_add_fusion.where_ref
  68.0 2.8 %direct.1.direct_ref = bf16[384,800]{1,0:T(8,128)(2,1)S(1)} custom-call(bf16[32,80,128]{2,1,0:T(8,128)(2,1)} %bitcast.5.pieces_ref), custom_call_target="tpu_custom_call" | custom-call | flops 629145600 | bytes 1228800 | tf_op jit(solution)/shard_map/direct/pallas_call | solution.py:158
  70.7 16.2 %all-to-all-done.1.pieces_ref = bf16[32,80,128]{2,1,0:T(8,128)(2,1)S(1)} async-done(((bf16[32,80,128]{2,1,0:T(8,128)(2,1)}), bf16[32,80,128]{2,1,0:T(8,128)(2,1)S(1)}, u32[]{:S(2)}, u32[]{:S(2)}) %all-to-all-start.1) | async-done | bytes 655392 | tf_op jit(solution)/shard_map/all_to_all | solution.py:155
  86.9 0.4 amplitude.1.amplitude_ref
  87.2 0.0 all-gather.2.cloned.1.call-done
  87.3 4.8 %contraction_sent.1 = bf16[150,800]{1,0:T(8,128)(2,1)S(1)} custom-call(s32[2]{0:T(128)S(1)} %pad_add_fusion.where_ref, bf16[384,800]{1,0:T(8,128)(2,1)S(1)} %amplitude.1.amplitude_ref, bf16[8,1696,256]{2,1,0:T(8,128)(2,1)} %bitcast.16), custom_call_target="tpu_custom_call" | custom-call | flops 960000000 | bytes 6946816 | tf_op jit(solution)/shard_map/contraction_sent/pallas_call | solution.py:183
  92.1 1.9 %collective-permute-start = (bf16[150,800]{1,0:T(8,128)(2,1)S(1)}, bf16[150,800]{1,0:T(8,128)(2,1)S(1)}, u32[]{:S(2)}, u32[]{:S(2)}) collective-permute-start(bf16[150,800]{1,0:T(8,128)(2,1)S(1)} %contraction_sent.1), channel_id=1, source_target_pairs={{0,1},{1,0},{2,3},{3,2},{4,5},{5,4},{6,7},{7,6},{8,9},{9,8},{10,11... | collective-permute-start | bytes 720008 | tf_op jit(solution)/shard_map/ppermute | solution.py:194
  94.0 4.8 %contraction_kept.1.own_ref = f32[150,800]{1,0:T(8,128)S(1)} custom-call(s32[2]{0:T(128)S(1)} %pad_add_fusion.where_ref, bf16[384,800]{1,0:T(8,128)(2,1)S(1)} %amplitude.1.amplitude_ref, bf16[8,1696,256]{2,1,0:T(8,128)(2,1)} %bitcast.17), custom_call_target="tpu_custom_call" | custom-call | flops 960000000 | bytes 6946816 | tf_op jit(solution)/shard_map/contraction_kept/pallas_call | solution.py:183
  98.8 12.3 %collective-permute-done.received_ref = bf16[150,800]{1,0:T(8,128)(2,1)S(1)} collective-permute-done((bf16[150,800]{1,0:T(8,128)(2,1)S(1)}, bf16[150,800]{1,0:T(8,128)(2,1)S(1)}, u32[]{:S(2)}, u32[]{:S(2)}) %collective-permute-start) | collective-permute-done | bytes 240032 | tf_op jit(solution)/shard_map/ppermute | solution.py:194
  111.1 0.9 finish.1
  (2 shorter events, 0.1 us)
Async XLA Ops:
  6.5 2.1 %copy-start = (bf16[96,25,50]{0,2,1:T(8,128)(2,1)S(1)}, bf16[96,25,50]{0,2,1:T(8,128)(2,1)}, u32[]{:S(2)}) copy-start(bf16[96,25,50]{0,2,1:T(8,128)(2,1)} %param.4) | copy-start | bytes 720004
  6.5 80.7 %all-gather.2.cloned.1.call-start = ((), (), s32[]{:S(2)}) async-start(), calls=%async_computation.2 | async-start | bytes 7380992 | tf_op jit(solution)/shard_map/all_gather | solution.py:146
  56.4 30.5 %all-to-all-start.1 = ((bf16[32,80,128]{2,1,0:T(8,128)(2,1)}), bf16[32,80,128]{2,1,0:T(8,128)(2,1)S(1)}, u32[]{:S(2)}, u32[]{:S(2)}) async-start(bf16[32,80,128]{2,1,0:T(8,128)(2,1)} %bitcast.5.pieces_ref), calls=%async_computation.1 | async-start | bytes 1310720 | tf_op jit(solution)/shard_map/all_to_all | solution.py:155
  92.1 19.0 %collective-permute-start = (bf16[150,800]{1,0:T(8,128)(2,1)S(1)}, bf16[150,800]{1,0:T(8,128)(2,1)S(1)}, u32[]{:S(2)}, u32[]{:S(2)}) collective-permute-start(bf16[150,800]{1,0:T(8,128)(2,1)S(1)} %contraction_sent.1), channel_id=1, source_target_pairs={{0,1},{1,0},{2,3},{3,2},{4,5},{5,4},{6,7},{7,6},{8,9},{9,8},{10,11... | collective-permute-start | bytes 720008 | tf_op jit(solution)/shard_map/ppermute | solution.py:194
Sparse Core Ops, SparseCore 0:
  9.5 70.0 all-gather.1

commit v5 on v4

v5 whole, which is shorter than its diff:
```python
import functools

import jax
import jax.numpy as jnp
from jax import lax
from jax.experimental import pallas as pl
from jax.experimental.pallas import tpu as pltpu
from jax.sharding import Mesh, PartitionSpec as P

ROWS, SLOT, LANES, FOLD = 25, 32, 128, 13
F32, BF16 = jnp.float32, jnp.bfloat16


def pack_kernel(core_ref, first_hbm, weights_hbm, second_hbm, out_ref, held, sems):
    virtual, block = first_hbm.shape
    half = weights_hbm.shape[0] // 2
    out_ref[:, LANES:] = jnp.zeros((out_ref.shape[0], out_ref.shape[1] - LANES), BF16)

    def fetch(big_hbm, big_at, small_from, small_at):
        big = pltpu.make_async_copy(big_hbm, held.at[pl.ds(big_at, virtual)], sems.at[0])
        small = pltpu.make_async_copy(weights_hbm.at[pl.ds(small_from, half)], held.at[pl.ds(small_at, half)], sems.at[1])
        big.start()
        small.start()
        big.wait()
        small.wait()

    @pl.when(core_ref[0] == 0)
    def _():
        fetch(first_hbm, 0, 0, virtual)

    @pl.when(core_ref[0] != 0)
    def _():
        fetch(second_hbm, half, half, 0)

    out_ref[:, :block] = held[...]


def unfold(whole):
    front, back = FOLD, ROWS - FOLD
    tail = jnp.concatenate([whole[ROWS : ROWS + front], pltpu.roll(whole[ROWS : ROWS + front], LANES // 2, 1)[:back]], 0)
    return [whole[:ROWS], tail]


def direct_kernel(pieces_ref, out_ref, wide_ref, pick_ref):
    count = pieces_ref.shape[0]
    orbitals = out_ref.shape[0] // SLOT
    depth, width = pick_ref.shape
    at = lax.broadcasted_iota(jnp.int32, (depth, width), 0)
    to = lax.broadcasted_iota(jnp.int32, (depth, width), 1)
    within = at % SLOT
    target = jnp.where(within < ROWS, (at // SLOT) * ROWS + within, -1)
    pick_ref[...] = jnp.where(target == to, 1.0, 0.0).astype(BF16)
    lane = lax.broadcasted_iota(jnp.int32, (ROWS, LANES), 1) // SLOT
    wide_ref[...] = jnp.zeros_like(wide_ref)
    for quad in range(count // 4):
        parts = [unfold(pieces_ref[4 * quad + k].astype(F32)) for k in range(4)]
        for orbital in range(orbitals):
            placed = None
            for k in range(4):
                shift = SLOT * ((k - orbital) % 4)
                part = parts[k][orbital // 4]
                moved = pltpu.roll(part, shift, 1) if shift else part
                placed = moved if placed is None else jnp.where(lane == k, moved, placed)
            wide_ref[orbital * SLOT : orbital * SLOT + ROWS, quad * LANES : (quad + 1) * LANES] = placed
    out_ref[...] = jnp.dot(wide_ref[...].astype(BF16), pick_ref[...], preferred_element_type=F32).astype(BF16)


def amplitude_kernel(direct_ref, pieces_ref, out_ref, flat_ref):
    count = pieces_ref.shape[0]
    orbitals = out_ref.shape[0] // ROWS
    for source in range(count):
        for group, part in enumerate(unfold(pieces_ref[source].astype(F32))):
            flat_ref[group, source * ROWS : (source + 1) * ROWS, :] = part
    rows = []
    for group in range(flat_ref.shape[0]):
        mirrored = jnp.transpose(flat_ref[group])
        for k in range(min(4, orbitals - 4 * group)):
            start = (4 * group + k) * SLOT
            rows.append(direct_ref[start : start + SLOT, :].astype(F32)[:ROWS] - mirrored[k * SLOT : k * SLOT + ROWS])
    out_ref[...] = jnp.concatenate(rows, 0).astype(BF16)


def contraction_kernel(first_ref, amplitude_ref, factors_hbm, out_ref, held, sems, *, orbitals):
    rows, depth = amplitude_ref.shape
    chunks = sems.shape[0]
    per = factors_hbm.shape[0] // chunks
    copies = [
        pltpu.make_async_copy(factors_hbm.at[pl.ds(j * per, per)], held.at[pl.ds(j * per, per)], sems.at[j])
        for j in range(chunks)
    ]
    for copy in copies:
        copy.start()
    begin = (lax.broadcasted_iota(jnp.int32, (rows, orbitals), 1) - first_ref[0]) * ROWS
    row = lax.broadcasted_iota(jnp.int32, (rows, orbitals), 0)
    pick = jnp.where((row >= begin) & (row < begin + ROWS), 1.0, 0.0).astype(BF16)
    amplitude = amplitude_ref[...]
    total = None
    for j in range(chunks):
        copies[j].wait()
        scaled, second = [], []
        for k in range(j * per, (j + 1) * per):
            value = jnp.dot(amplitude, held[k, :depth], preferred_element_type=F32)
            scale = jnp.dot(pick, held[k, depth : depth + orbitals], preferred_element_type=F32)
            scaled.append((value * scale).astype(BF16))
            second.append(held[k, depth + orbitals : 2 * depth + orbitals])
        part = lax.dot_general(
            jnp.concatenate(scaled, 1), jnp.concatenate(second, 1), (((1,), (1,)), ((), ())), preferred_element_type=F32
        )
        total = part if total is None else total + part
    out_ref[...] = total.astype(out_ref.dtype)


def finish_kernel(own_ref, received_ref, out_ref):
    received = received_ref[...].astype(F32)
    for k in range(out_ref.shape[0]):
        rows = slice(k * ROWS, (k + 1) * ROWS)
        out_ref[k] = (own_ref[rows] + received[rows]).astype(BF16)


def vmem(count):
    return [pl.BlockSpec(memory_space=pltpu.VMEM)] * count


def hbm(count):
    return [pl.BlockSpec(memory_space=pltpu.HBM)] * count


SMEM = [pl.BlockSpec(memory_space=pltpu.SMEM)]
ROOM = pltpu.CompilerParams(vmem_limit_bytes=32 * 2**20)
SMALL = pltpu.CompilerParams(vmem_limit_bytes=16 * 2**20)
BIG = pltpu.CompilerParams(vmem_limit_bytes=48 * 2**20)
FULL = pltpu.CompilerParams(vmem_limit_bytes=60 * 2**20)


def body(halves, first_factor, second_factor, weights):
    y_count, row_count = lax.axis_size("y"), lax.axis_size("p") * 2
    orbitals = halves.shape[0]
    block, virtual = first_factor.shape
    columns = 2 * y_count
    local = orbitals // columns
    column, core = lax.axis_index(("y", "zh")), lax.axis_index("c")

    lanes = (block + LANES - 1) // LANES * LANES
    half = virtual + orbitals // 2
    share = pl.pallas_call(
        pack_kernel,
        in_specs=SMEM + hbm(3),
        out_specs=vmem(1)[0],
        out_shape=jax.ShapeDtypeStruct((half, lanes), BF16),
        scratch_shapes=[pltpu.VMEM((half, block), BF16), pltpu.SemaphoreType.DMA((2,))],
        compiler_params=FULL,
        name="pack",
    )(core.reshape(1), first_factor.T, weights.T, second_factor.T)
    factors = lax.all_gather(share, ("y", "c"), axis=0, tiled=True).reshape(y_count, 2 * half, lanes)

    height = (ROWS + FOLD + 7) // 8 * 8
    split = halves.reshape(columns, local, ROWS, 2, ROWS).transpose(0, 3, 2, 1, 4)
    split = jnp.pad(split, ((0, 0),) * 4 + ((0, SLOT - ROWS),))
    four = split[:, :, :, :4].reshape(columns, 2, ROWS, LANES)
    two = split[:, :, :, 4:].reshape(columns, 2, ROWS, LANES // 2)
    fold = jnp.pad(two[:, :, FOLD:], ((0, 0), (0, 0), (0, 2 * FOLD - ROWS), (0, 0)))
    two = jnp.concatenate([two[:, :, :FOLD], fold], 3)
    spare = jnp.zeros((columns, 2, height - ROWS - FOLD, LANES), BF16)
    pieces = jnp.concatenate([four, two, spare], 2)
    direct = lax.all_to_all(pieces, ("y", "zh"), 0, 0, tiled=True).reshape(row_count, height, LANES)
    mirrored = lax.all_to_all(direct, ("p", "c"), 0, 0, tiled=True)
    slots, rows = local * SLOT, local * ROWS
    direct = pl.pallas_call(
        direct_kernel,
        in_specs=vmem(1),
        out_specs=vmem(1)[0],
        out_shape=jax.ShapeDtypeStruct((slots, virtual), BF16),
        scratch_shapes=[pltpu.VMEM((slots, row_count * SLOT), F32), pltpu.VMEM((row_count * SLOT, virtual), BF16)],
        compiler_params=ROOM,
        cost_estimate=pl.CostEstimate(flops=2 * slots * row_count * SLOT * virtual, bytes_accessed=4 * slots * virtual, transcendentals=0),
        name="direct",
    )(direct)
    amplitude = pl.pallas_call(
        amplitude_kernel,
        in_specs=vmem(2),
        out_specs=vmem(1)[0],
        out_shape=jax.ShapeDtypeStruct((rows, virtual), BF16),
        scratch_shapes=[pltpu.VMEM((2, virtual, LANES), F32)],
        compiler_params=ROOM,
        name="amplitude",
    )(direct, mirrored)

    chunks = max(y_count // 2, 1)

    def contraction(name, first, amplitude, dtype):
        return pl.pallas_call(
            functools.partial(contraction_kernel, orbitals=orbitals),
            in_specs=SMEM + vmem(1) + hbm(1),
            out_specs=vmem(1)[0],
            out_shape=jax.ShapeDtypeStruct((rows, virtual), dtype),
            scratch_shapes=[pltpu.VMEM((y_count, 2 * half, lanes), BF16), pltpu.SemaphoreType.DMA((chunks,))],
            compiler_params=BIG,
            cost_estimate=pl.CostEstimate(flops=rows * virtual * block * y_count * 4, bytes_accessed=y_count * 4 * half * lanes, transcendentals=0),
            name=name,
        )(first.reshape(1), amplitude, factors)

    swap = [(0, 1), (1, 0)]
    partner = column + 1 - 2 * lax.axis_index("zh")
    theirs = lax.ppermute(amplitude, "zh", swap)
    received = lax.ppermute(contraction("contraction_sent", partner * local, theirs, BF16), "zh", swap)
    kept = contraction("contraction_kept", column * local, amplitude, F32)
    return pl.pallas_call(
        finish_kernel,
        in_specs=vmem(2),
        out_specs=vmem(1)[0],
        out_shape=jax.ShapeDtypeStruct((local, ROWS, virtual), BF16),
        compiler_params=SMALL,
        name="finish",
    )(kept, received)


def solution(mesh):
    rows, columns = mesh.devices.shape
    fine = Mesh(mesh.devices.reshape(rows // 2, 2, columns // 2, 2), ("p", "c", "y", "zh"))
    row, col = ("p", "c"), ("y", "zh")
    placed = (P(None, row, col), P(col, None), P(col, None), P(col, None))
    return jax.shard_map(body, mesh=fine, in_specs=placed, out_specs=P(col, row, None), check_vma=False)
```

time: 119 us -> 118 us (level)
  the two profiles are of different devices: /device:TPU:1 before, /device:TPU:3 now
where the time goes in v5:
time: 118 us
  waiting for transfers between devices  38.1 us (32%)
  blocking collectives  34.5 us (29%)
  starting transfers between devices  14.4 us (12%)
  Pallas kernels  13.6 us (12%)
  between operations  13.6 us (12%)
  local copies, waits for them, and re-layouts  3.69 us (3%)
    all_to_all x1, blocking collectives, body(): lax.all_to_all(pieces, ('y', 'zh'), 0, 0, tiled=True)  34.5 us
    ppermute x1, waiting for transfers between devices, body(): theirs = lax.ppermute(amplitude, 'zh', swap)  15.9 us
    ppermute x1, waiting for transfers between devices, body(): lax.ppermute(contraction('contraction_sent', partner * local, theirs, BF1...  12.9 us
    all_to_all x1, starting transfers between devices, body(): mirrored = lax.all_to_all(direct, ('p', 'c'), 0, 0, tiled=True)  10.5 us
    all_to_all x1, waiting for transfers between devices, body(): mirrored = lax.all_to_all(direct, ('p', 'c'), 0, 0, tiled=True)  9.26 us
    pallas_call x2, Pallas kernels, contraction(): pl.pallas_call(functools.partial(contraction_kernel, orbitals=orbitals),...  8.38 us
  transfers between devices with their start and end apart: 4, of which 3 were waited for; matrix products, arithmetic and copies ran while one was open for 3% of the time, Pallas kernels for 6%

profile of v5, /device:TPU:3, one launch (start us, length us, event | category | flops | bytes accessed | tf_op | source)
XLA Modules:
  0.0 118.0 jit_solution(1525876292481507000)
XLA Ops:
  6.5 0.0 copy-start
  6.5 0.0 all-gather.2.cloned.1.call-start
  6.5 1.9 %pack.1 = bf16[848,256]{1,0:T(8,128)(2,1)} custom-call(s32[1]{0:T(128)} %bitcast.3.core_ref, bf16[800,250]{1,0:T(8,128)(2,1)} %bitcast.19, bf16[96,250]{1,0:T(8,128)(2,1)} %bitcast.21, bf16[800,250]{1,0:T(8,128)(2,1)} %bitcast.20), custom_call_target="tpu_custom_call" | custom-call | tf_op jit(solution)/shard_map/pack/pallas_call | solution.py:145
  8.4 0.0 all-gather.2.cloned.1.call-update
  8.5 0.0 copy-done
  8.5 0.4 copy.11
  8.8 0.5 reshape.25
  9.3 0.5 pad_slice_fusion
  9.8 0.2 copy.13
  10.0 0.2 reshape.27
  10.3 1.0 pad_slice_fusion.1
  11.2 0.4 copy.12
  11.6 0.4 reshape.26
  12.1 0.1 pad.13.clone
  12.1 0.2 fusion.6
  12.3 0.1 copy.14
  12.4 34.5 %all_to_all.10 = bf16[16,2,40,128]{3,2,1,0:T(8,128)(2,1)} all-to-all(bf16[16,2,40,128]{3,2,1,0:T(8,128)(2,1)S(1)} %copy.14), channel_id=1, replica_groups=mesh['p'=16,'c'=2,'y'=8,'zh'=2] {'y','zh'}, dimensions={0} | all-to-all | bytes 655360 | tf_op jit(solution)/shard_map/all_to_all | solution.py:165
  46.9 10.5 %all-to-all-start.1 = ((bf16[32,40,128]{2,1,0:T(8,128)(2,1)}), bf16[32,40,128]{2,1,0:T(8,128)(2,1)S(1)}, u32[]{:S(2)}, u32[]{:S(2)}) async-start(bf16[32,40,128]{2,1,0:T(8,128)(2,1)} %bitcast.2.pieces_ref), calls=%async_computation.1 | async-start | bytes 655360 | tf_op jit(solution)/shard_map/all_to_all | solution.py:166
  57.5 2.2 %direct.1.direct_ref = bf16[192,800]{1,0:T(8,128)(2,1)S(1)} custom-call(bf16[32,40,128]{2,1,0:T(8,128)(2,1)} %bitcast.2.pieces_ref), custom_call_target="tpu_custom_call" | custom-call | flops 314572800 | bytes 614400 | tf_op jit(solution)/shard_map/direct/pallas_call | solution.py:168
  59.7 9.3 %all-to-all-done.1.pieces_ref = bf16[32,40,128]{2,1,0:T(8,128)(2,1)S(1)} async-done(((bf16[32,40,128]{2,1,0:T(8,128)(2,1)}), bf16[32,40,128]{2,1,0:T(8,128)(2,1)S(1)}, u32[]{:S(2)}, u32[]{:S(2)}) %all-to-all-start.1) | async-done | bytes 327712 | tf_op jit(solution)/shard_map/all_to_all | solution.py:166
  69.0 0.3 amplitude.1.amplitude_ref
  69.2 1.9 %collective-permute-start = (bf16[150,800]{1,0:T(8,128)(2,1)S(1)}, bf16[150,800]{1,0:T(8,128)(2,1)S(1)}, u32[]{:S(2)}, u32[]{:S(2)}) collective-permute-start(bf16[150,800]{1,0:T(8,128)(2,1)S(1)} %amplitude.1.amplitude_ref), channel_id=1, source_target_pairs={{0,1},{1,0},{2,3},{3,2},{4,5},{5,4},{6,7},{7,6},{8,9},{9,8},{10,11... | collective-permute-start | bytes 720008 | tf_op jit(solution)/shard_map/ppermute | solution.py:204
  71.2 15.9 %collective-permute-done.amplitude_ref = bf16[150,800]{1,0:T(8,128)(2,1)S(1)} collective-permute-done((bf16[150,800]{1,0:T(8,128)(2,1)S(1)}, bf16[150,800]{1,0:T(8,128)(2,1)S(1)}, u32[]{:S(2)}, u32[]{:S(2)}) %collective-permute-start) | collective-permute-done | bytes 240032 | tf_op jit(solution)/shard_map/ppermute | solution.py:204
  87.1 0.0 all-gather.2.cloned.1.call-done
  87.1 4.2 %contraction_sent.1 = bf16[150,800]{1,0:T(8,128)(2,1)S(1)} custom-call(s32[1]{0:T(128)} %bitcast.8.first_ref, bf16[150,800]{1,0:T(8,128)(2,1)S(1)} %collective-permute-done.amplitude_ref, bf16[8,1696,256]{2,1,0:T(8,128)(2,1)} %bitcast.15), custom_call_target="tpu_custom_call" | custom-call | flops 960000000 | bytes 6946816 | tf_op jit(solution)/shard_map/contraction_sent/pallas_call | solution.py:191
  91.3 1.9 %collective-permute-start.1 = (bf16[150,800]{1,0:T(8,128)(2,1)S(1)}, bf16[150,800]{1,0:T(8,128)(2,1)S(1)}, u32[]{:S(2)}, u32[]{:S(2)}) collective-permute-start(bf16[150,800]{1,0:T(8,128)(2,1)S(1)} %contraction_sent.1), channel_id=1, source_target_pairs={{0,1},{1,0},{2,3},{3,2},{4,5},{5,4},{6,7},{7,6},{8,9},{9,8},{10,11... | collective-permute-start | bytes 720008 | tf_op jit(solution)/shard_map/ppermute | solution.py:205
  93.2 4.2 %contraction_kept.1.own_ref = f32[150,800]{1,0:T(8,128)S(1)} custom-call(s32[1]{0:T(128)} %bitcast.first_ref, bf16[150,800]{1,0:T(8,128)(2,1)S(1)} %amplitude.1.amplitude_ref, bf16[8,1696,256]{2,1,0:T(8,128)(2,1)} %bitcast.16), custom_call_target="tpu_custom_call" | custom-call | flops 960000000 | bytes 6946816 | tf_op jit(solution)/shard_map/contraction_kept/pallas_call | solution.py:191
  97.4 12.9 %collective-permute-done.1.received_ref = bf16[150,800]{1,0:T(8,128)(2,1)S(1)} collective-permute-done((bf16[150,800]{1,0:T(8,128)(2,1)S(1)}, bf16[150,800]{1,0:T(8,128)(2,1)S(1)}, u32[]{:S(2)}, u32[]{:S(2)}) %collective-permute-start.1) | collective-permute-done | bytes 240032 | tf_op jit(solution)/shard_map/ppermute | solution.py:205
  110.3 0.9 finish.1
  (3 shorter events, 0.0 us)
Async XLA Ops:
  6.5 1.9 %copy-start = (bf16[96,25,50]{0,2,1:T(8,128)(2,1)S(1)}, bf16[96,25,50]{0,2,1:T(8,128)(2,1)}, u32[]{:S(2)}) copy-start(bf16[96,25,50]{0,2,1:T(8,128)(2,1)} %param.4) | copy-start | bytes 720004
  6.5 80.5 %all-gather.2.cloned.1.call-start = ((), (), s32[]{:S(2)}) async-start(), calls=%async_computation.2 | async-start | bytes 7380992 | tf_op jit(solution)/shard_map/all_gather | solution.py:154
  46.9 22.0 %all-to-all-start.1 = ((bf16[32,40,128]{2,1,0:T(8,128)(2,1)}), bf16[32,40,128]{2,1,0:T(8,128)(2,1)S(1)}, u32[]{:S(2)}, u32[]{:S(2)}) async-start(bf16[32,40,128]{2,1,0:T(8,128)(2,1)} %bitcast.2.pieces_ref), calls=%async_computation.1 | async-start | bytes 655360 | tf_op jit(solution)/shard_map/all_to_all | solution.py:166
  69.2 17.8 %collective-permute-start = (bf16[150,800]{1,0:T(8,128)(2,1)S(1)}, bf16[150,800]{1,0:T(8,128)(2,1)S(1)}, u32[]{:S(2)}, u32[]{:S(2)}) collective-permute-start(bf16[150,800]{1,0:T(8,128)(2,1)S(1)} %amplitude.1.amplitude_ref), channel_id=1, source_target_pairs={{0,1},{1,0},{2,3},{3,2},{4,5},{5,4},{6,7},{7,6},{8,9},{9,8},{10,11... | collective-permute-start | bytes 720008 | tf_op jit(solution)/shard_map/ppermute | solution.py:204
  91.3 19.1 %collective-permute-start.1 = (bf16[150,800]{1,0:T(8,128)(2,1)S(1)}, bf16[150,800]{1,0:T(8,128)(2,1)S(1)}, u32[]{:S(2)}, u32[]{:S(2)}) collective-permute-start(bf16[150,800]{1,0:T(8,128)(2,1)S(1)} %contraction_sent.1), channel_id=1, source_target_pairs={{0,1},{1,0},{2,3},{3,2},{4,5},{5,4},{6,7},{7,6},{8,9},{9,8},{10,11... | collective-permute-start | bytes 720008 | tf_op jit(solution)/shard_map/ppermute | solution.py:205
Sparse Core Ops, SparseCore 0:
  9.5 63.4 all-gather.1

commit v6 on v5

--- a/solution.py
+++ b/solution.py
@@ -43,7 +43,7 @@
 
 def direct_kernel(pieces_ref, out_ref, wide_ref, pick_ref):
     count = pieces_ref.shape[0]
-    orbitals = out_ref.shape[0] // SLOT
+    orbitals = out_ref.shape[0] // ROWS
     depth, width = pick_ref.shape
     at = lax.broadcasted_iota(jnp.int32, (depth, width), 0)
     to = lax.broadcasted_iota(jnp.int32, (depth, width), 1)
@@ -62,22 +62,22 @@
                 moved = pltpu.roll(part, shift, 1) if shift else part
                 placed = moved if placed is None else jnp.where(lane == k, moved, placed)
             wide_ref[orbital * SLOT : orbital * SLOT + ROWS, quad * LANES : (quad + 1) * LANES] = placed
-    out_ref[...] = jnp.dot(wide_ref[...].astype(BF16), pick_ref[...], preferred_element_type=F32).astype(BF16)
-
-
-def amplitude_kernel(direct_ref, pieces_ref, out_ref, flat_ref):
+    laid = jnp.dot(wide_ref[...].astype(BF16), pick_ref[...], preferred_element_type=F32)
+    out_ref[...] = jnp.concatenate([laid[k * SLOT : k * SLOT + ROWS] for k in range(orbitals)], 0).astype(BF16)
+
+
+def amplitude_kernel(side_ref, direct_ref, pieces_ref, out_ref, flat_ref):
     count = pieces_ref.shape[0]
     orbitals = out_ref.shape[0] // ROWS
     for source in range(count):
-        for group, part in enumerate(unfold(pieces_ref[source].astype(F32))):
+        for group, part in enumerate(unfold(pieces_ref[source, side_ref[0]].astype(F32))):
             flat_ref[group, source * ROWS : (source + 1) * ROWS, :] = part
     rows = []
     for group in range(flat_ref.shape[0]):
         mirrored = jnp.transpose(flat_ref[group])
         for k in range(min(4, orbitals - 4 * group)):
-            start = (4 * group + k) * SLOT
-            rows.append(direct_ref[start : start + SLOT, :].astype(F32)[:ROWS] - mirrored[k * SLOT : k * SLOT + ROWS])
-    out_ref[...] = jnp.concatenate(rows, 0).astype(BF16)
+            rows.append(mirrored[k * SLOT : k * SLOT + ROWS])
+    out_ref[...] = (direct_ref[...].astype(F32) - jnp.concatenate(rows, 0)).astype(BF16)
 
 
 def contraction_kernel(first_ref, amplitude_ref, factors_hbm, out_ref, held, sems, *, orbitals):
@@ -163,27 +163,31 @@
     spare = jnp.zeros((columns, 2, height - ROWS - FOLD, LANES), BF16)
     pieces = jnp.concatenate([four, two, spare], 2)
     direct = lax.all_to_all(pieces, ("y", "zh"), 0, 0, tiled=True).reshape(row_count, height, LANES)
-    mirrored = lax.all_to_all(direct, ("p", "c"), 0, 0, tiled=True)
+    both = jnp.broadcast_to(direct[:, None], (row_count, 2, height, LANES)).reshape(2 * row_count, height, LANES)
+    mirrored = lax.all_to_all(both, ("p", "c", "zh"), 0, 0, tiled=True).reshape(row_count, 2, height, LANES)
     slots, rows = local * SLOT, local * ROWS
+    laid = jax.ShapeDtypeStruct((rows, virtual), BF16)
     direct = pl.pallas_call(
         direct_kernel,
         in_specs=vmem(1),
         out_specs=vmem(1)[0],
-        out_shape=jax.ShapeDtypeStruct((slots, virtual), BF16),
+        out_shape=laid,
         scratch_shapes=[pltpu.VMEM((slots, row_count * SLOT), F32), pltpu.VMEM((row_count * SLOT, virtual), BF16)],
         compiler_params=ROOM,
         cost_estimate=pl.CostEstimate(flops=2 * slots * row_count * SLOT * virtual, bytes_accessed=4 * slots * virtual, transcendentals=0),
         name="direct",
     )(direct)
-    amplitude = pl.pallas_call(
-        amplitude_kernel,
-        in_specs=vmem(2),
-        out_specs=vmem(1)[0],
-        out_shape=jax.ShapeDtypeStruct((rows, virtual), BF16),
-        scratch_shapes=[pltpu.VMEM((2, virtual, LANES), F32)],
-        compiler_params=ROOM,
-        name="amplitude",
-    )(direct, mirrored)
+
+    def amplitude(name, side, direct):
+        return pl.pallas_call(
+            amplitude_kernel,
+            in_specs=SMEM + vmem(2),
+            out_specs=vmem(1)[0],
+            out_shape=laid,
+            scratch_shapes=[pltpu.VMEM((2, virtual, LANES), F32)],
+            compiler_params=ROOM,
+            name=name,
+        )(side.reshape(1), direct, mirrored)
 
     chunks = max(y_count // 2, 1)
 
@@ -200,10 +204,12 @@
         )(first.reshape(1), amplitude, factors)
 
     swap = [(0, 1), (1, 0)]
-    partner = column + 1 - 2 * lax.axis_index("zh")
-    theirs = lax.ppermute(amplitude, "zh", swap)
+    side = lax.axis_index("zh")
+    partner = column + 1 - 2 * side
+    theirs = amplitude("amplitude_sent", 1 - side, lax.ppermute(direct, "zh", swap))
     received = lax.ppermute(contraction("contraction_sent", partner * local, theirs, BF16), "zh", swap)
-    kept = contraction("contraction_kept", column * local, amplitude, F32)
+    ours = amplitude("amplitude_kept", side, direct)
+    kept = contraction("contraction_kept", column * local, ours, F32)
     return pl.pallas_call(
         finish_kernel,
         in_specs=vmem(2),

time: 118 us -> 120 us (1.017)
  the two profiles are of different devices: /device:TPU:3 before, /device:TPU:67 now
where the time goes in v6:
time: 120 us
  waiting for transfers between devices  35 us (29%)
  blocking collectives  34.1 us (28%)
  starting transfers between devices  19.4 us (16%)
  between operations  13.6 us (11%)
  Pallas kernels  12.8 us (11%)
  local copies, waits for them, and re-layouts  4.6 us (4%)
    all_to_all x1, blocking collectives, body(): lax.all_to_all(pieces, ('y', 'zh'), 0, 0, tiled=True)  34.1 us
    ppermute x1, waiting for transfers between devices, body(): lax.ppermute(direct, 'zh', swap)  23.3 us
    ppermute x1, waiting for transfers between devices, body(): lax.ppermute(contraction('contraction_sent', partner * local, theirs, BF1...  11.7 us
    all_to_all x1, starting transfers between devices, body(): lax.all_to_all(both, ('p', 'c', 'zh'), 0, 0, tiled=True)  10.4 us
    pallas_call x2, Pallas kernels, contraction(): pl.pallas_call(functools.partial(contraction_kernel, orbitals=orbitals),...  8.39 us
    ppermute x1, starting transfers between devices, body(): lax.ppermute(direct, 'zh', swap)  6.11 us
    ppermute x1, starting transfers between devices, body(): lax.ppermute(contraction('contraction_sent', partner * local, theirs, BF1...  2.89 us
  transfers between devices with their start and end apart: 4, of which 2 were waited for; matrix products, arithmetic and copies ran while one was open for 4% of the time, Pallas kernels for 5%

profile of v6, /device:TPU:67, one launch (start us, length us, event | category | flops | bytes accessed | tf_op | source)
XLA Modules:
  0.0 119.7 jit_solution(3241247995463920382)
XLA Ops:
  6.5 0.0 copy-start
  6.5 0.0 all-gather.2.cloned.1.call-start
  6.5 1.9 %pack.1 = bf16[848,256]{1,0:T(8,128)(2,1)} custom-call(s32[1]{0:T(128)} %bitcast.6.core_ref, bf16[800,250]{1,0:T(8,128)(2,1)} %bitcast.27, bf16[96,250]{1,0:T(8,128)(2,1)} %bitcast.29, bf16[800,250]{1,0:T(8,128)(2,1)} %bitcast.28), custom_call_target="tpu_custom_call" | custom-call | tf_op jit(solution)/shard_map/pack/pallas_call | solution.py:145
  8.4 0.0 all-gather.2.cloned.1.call-update
  8.5 0.0 copy-done
  8.5 0.4 copy.11
  8.8 0.5 reshape.39
  9.3 0.5 pad_slice_fusion
  9.8 0.2 copy.13
  10.0 0.2 reshape.41
  10.3 1.0 pad_slice_fusion.1
  11.2 0.4 copy.12
  11.6 0.4 reshape.40
  12.1 0.1 pad.13.clone
  12.1 0.2 fusion.6
  12.3 0.1 copy.14
  12.4 34.1 %all_to_all.10 = bf16[16,2,40,128]{3,2,1,0:T(8,128)(2,1)S(1)} all-to-all(bf16[16,2,40,128]{3,2,1,0:T(8,128)(2,1)S(1)} %copy.14), channel_id=1, replica_groups=mesh['p'=16,'c'=2,'y'=8,'zh'=2] {'y','zh'}, dimensions={0} | all-to-all | bytes 655360 | tf_op jit(solution)/shard_map/all_to_all | solution.py:165
  46.5 0.9 broadcast_in_dim.9
  47.4 10.4 %all-to-all-start.1 = ((bf16[64,40,128]{2,1,0:T(8,128)(2,1)}), bf16[64,40,128]{2,1,0:T(8,128)(2,1)S(1)}, u32[]{:S(2)}, u32[]{:S(2)}) async-start(bf16[64,40,128]{2,1,0:T(8,128)(2,1)} %bitcast.4), calls=%async_computation.1 | async-start | bytes 1310720 | tf_op jit(solution)/shard_map/all_to_all | solution.py:167
  57.8 1.2 direct.1.direct_ref
  59.0 6.1 %collective-permute-start = (bf16[150,800]{1,0:T(8,128)(2,1)S(1)}, bf16[150,800]{1,0:T(8,128)(2,1)S(1)}, u32[]{:S(2)}, u32[]{:S(2)}) collective-permute-start(bf16[150,800]{1,0:T(8,128)(2,1)S(1)} %direct.1.direct_ref), channel_id=1, source_target_pairs={{0,1},{1,0},{2,3},{3,2},{4,5},{5,4},{6,7},{7,6},{8,9},{9,8},{10,11... | collective-permute-start | bytes 720008 | tf_op jit(solution)/shard_map/ppermute | solution.py:209
  65.1 23.3 %collective-permute-done.direct_ref = bf16[150,800]{1,0:T(8,128)(2,1)S(1)} collective-permute-done((bf16[150,800]{1,0:T(8,128)(2,1)S(1)}, bf16[150,800]{1,0:T(8,128)(2,1)S(1)}, u32[]{:S(2)}, u32[]{:S(2)}) %collective-permute-start) | collective-permute-done | bytes 240032 | tf_op jit(solution)/shard_map/ppermute | solution.py:209
  88.5 0.0 all-to-all-done.1
  88.5 0.2 amplitude_sent.1.amplitude_ref
  88.7 0.0 all-gather.2.cloned.1.call-done
  88.7 4.2 %contraction_sent.1 = bf16[150,800]{1,0:T(8,128)(2,1)S(1)} custom-call(s32[1]{0:T(128)} %bitcast.11.first_ref, bf16[150,800]{1,0:T(8,128)(2,1)S(1)} %amplitude_sent.1.amplitude_ref, bf16[8,1696,256]{2,1,0:T(8,128)(2,1)} %bitcast.23), custom_call_target="tpu_custom_call" | custom-call | flops 960000000 | bytes 6946816 | tf_op jit(solution)/shard_map/contraction_sent/pallas_call | solution.py:195
  92.9 2.9 %collective-permute-start.1 = (bf16[150,800]{1,0:T(8,128)(2,1)S(1)}, bf16[150,800]{1,0:T(8,128)(2,1)S(1)}, u32[]{:S(2)}, u32[]{:S(2)}) collective-permute-start(bf16[150,800]{1,0:T(8,128)(2,1)S(1)} %contraction_sent.1), channel_id=1, source_target_pairs={{0,1},{1,0},{2,3},{3,2},{4,5},{5,4},{6,7},{7,6},{8,9},{9,8},{10,11... | collective-permute-start | bytes 720008 | tf_op jit(solution)/shard_map/ppermute | solution.py:210
  95.8 0.3 amplitude_kept.1.amplitude_ref
  96.1 4.2 %contraction_kept.1.own_ref = f32[150,800]{1,0:T(8,128)S(1)} custom-call(s32[1]{0:T(128)} %bitcast.first_ref, bf16[150,800]{1,0:T(8,128)(2,1)S(1)} %amplitude_kept.1.amplitude_ref, bf16[8,1696,256]{2,1,0:T(8,128)(2,1)} %bitcast.24), custom_call_target="tpu_custom_call" | custom-call | flops 960000000 | bytes 6946816 | tf_op jit(solution)/shard_map/contraction_kept/pallas_call | solution.py:195
  100.3 11.7 %collective-permute-done.1.received_ref = bf16[150,800]{1,0:T(8,128)(2,1)S(1)} collective-permute-done((bf16[150,800]{1,0:T(8,128)(2,1)S(1)}, bf16[150,800]{1,0:T(8,128)(2,1)S(1)}, u32[]{:S(2)}, u32[]{:S(2)}) %collective-permute-start.1) | collective-permute-done | bytes 240032 | tf_op jit(solution)/shard_map/ppermute | solution.py:210
  112.0 0.9 finish.1
  (3 shorter events, 0.0 us)
Async XLA Ops:
  6.5 1.9 %copy-start = (bf16[96,25,50]{0,2,1:T(8,128)(2,1)S(1)}, bf16[96,25,50]{0,2,1:T(8,128)(2,1)}, u32[]{:S(2)}) copy-start(bf16[96,25,50]{0,2,1:T(8,128)(2,1)} %param.4) | copy-start | bytes 720004
  6.5 82.2 %all-gather.2.cloned.1.call-start = ((), (), s32[]{:S(2)}) async-start(), calls=%async_computation.2 | async-start | bytes 7380992 | tf_op jit(solution)/shard_map/all_gather | solution.py:154
  47.4 41.0 %all-to-all-start.1 = ((bf16[64,40,128]{2,1,0:T(8,128)(2,1)}), bf16[64,40,128]{2,1,0:T(8,128)(2,1)S(1)}, u32[]{:S(2)}, u32[]{:S(2)}) async-start(bf16[64,40,128]{2,1,0:T(8,128)(2,1)} %bitcast.4), calls=%async_computation.1 | async-start | bytes 1310720 | tf_op jit(solution)/shard_map/all_to_all | solution.py:167
  59.0 29.5 %collective-permute-start = (bf16[150,800]{1,0:T(8,128)(2,1)S(1)}, bf16[150,800]{1,0:T(8,128)(2,1)S(1)}, u32[]{:S(2)}, u32[]{:S(2)}) collective-permute-start(bf16[150,800]{1,0:T(8,128)(2,1)S(1)} %direct.1.direct_ref), channel_id=1, source_target_pairs={{0,1},{1,0},{2,3},{3,2},{4,5},{5,4},{6,7},{7,6},{8,9},{9,8},{10,11... | collective-permute-start | bytes 720008 | tf_op jit(solution)/shard_map/ppermute | solution.py:209
  92.9 19.0 %collective-permute-start.1 = (bf16[150,800]{1,0:T(8,128)(2,1)S(1)}, bf16[150,800]{1,0:T(8,128)(2,1)S(1)}, u32[]{:S(2)}, u32[]{:S(2)}) collective-permute-start(bf16[150,800]{1,0:T(8,128)(2,1)S(1)} %contraction_sent.1), channel_id=1, source_target_pairs={{0,1},{1,0},{2,3},{3,2},{4,5},{5,4},{6,7},{7,6},{8,9},{9,8},{10,11... | collective-permute-start | bytes 720008 | tf_op jit(solution)/shard_map/ppermute | solution.py:210
Sparse Core Ops, SparseCore 0:
  9.5 62.5 all-gather.1

commit v7 on v5

--- a/solution.py
+++ b/solution.py
@@ -65,7 +65,37 @@
     out_ref[...] = jnp.dot(wide_ref[...].astype(BF16), pick_ref[...], preferred_element_type=F32).astype(BF16)
 
 
-def amplitude_kernel(direct_ref, pieces_ref, out_ref, flat_ref):
+def packed_height(rows, width):
+    full, tail = divmod(width, LANES)
+    stride = -(-rows // 8) * 8
+    per = LANES // tail if tail else 1
+    deep = -(-rows // per) if tail else 0
+    return full, tail, stride, per, deep, full * stride + -(-deep // 8) * 8
+
+
+def store_packed(out_ref, value):
+    rows, width = value.shape
+    full, tail, stride, per, deep, _ = packed_height(rows, width)
+    for j in range(full):
+        out_ref[j * stride : j * stride + rows, :] = value[:, j * LANES : (j + 1) * LANES].astype(out_ref.dtype)
+    if tail:
+        rest = value[:, full * LANES :]
+        if per * deep > rows:
+            rest = jnp.concatenate([rest, jnp.zeros((per * deep - rows, tail), F32)], 0)
+        rest = jnp.concatenate([rest[k * deep : (k + 1) * deep] for k in range(per)], 1)
+        out_ref[full * stride : full * stride + deep, : per * tail] = rest.astype(out_ref.dtype)
+
+
+def load_packed(ref, rows, width):
+    full, tail, stride, per, deep, _ = packed_height(rows, width)
+    parts = [ref[j * stride : j * stride + rows, :].astype(F32) for j in range(full)]
+    if tail:
+        rest = ref[full * stride : full * stride + deep, :].astype(F32)
+        parts.append(jnp.concatenate([rest[:, k * tail : (k + 1) * tail] for k in range(per)], 0)[:rows])
+    return jnp.concatenate(parts, 1)
+
+
+def amplitude_kernel(direct_ref, pieces_ref, out_ref, packed_ref, flat_ref):
     count = pieces_ref.shape[0]
     orbitals = out_ref.shape[0] // ROWS
     for source in range(count):
@@ -77,11 +107,12 @@
         for k in range(min(4, orbitals - 4 * group)):
             start = (4 * group + k) * SLOT
             rows.append(direct_ref[start : start + SLOT, :].astype(F32)[:ROWS] - mirrored[k * SLOT : k * SLOT + ROWS])
-    out_ref[...] = jnp.concatenate(rows, 0).astype(BF16)
-
-
-def contraction_kernel(first_ref, amplitude_ref, factors_hbm, out_ref, held, sems, *, orbitals):
-    rows, depth = amplitude_ref.shape
+    value = jnp.concatenate(rows, 0)
+    out_ref[...] = value.astype(BF16)
+    store_packed(packed_ref, value)
+
+
+def contraction_kernel(first_ref, amplitude_ref, factors_hbm, out_ref, held, sems, *, orbitals, rows, depth, packed):
     chunks = sems.shape[0]
     per = factors_hbm.shape[0] // chunks
     copies = [
@@ -93,7 +124,7 @@
     begin = (lax.broadcasted_iota(jnp.int32, (rows, orbitals), 1) - first_ref[0]) * ROWS
     row = lax.broadcasted_iota(jnp.int32, (rows, orbitals), 0)
     pick = jnp.where((row >= begin) & (row < begin + ROWS), 1.0, 0.0).astype(BF16)
-    amplitude = amplitude_ref[...]
+    amplitude = load_packed(amplitude_ref, rows, depth).astype(BF16) if packed else amplitude_ref[...]
     total = None
     for j in range(chunks):
         copies[j].wait()
@@ -107,14 +138,16 @@
             jnp.concatenate(scaled, 1), jnp.concatenate(second, 1), (((1,), (1,)), ((), ())), preferred_element_type=F32
         )
         total = part if total is None else total + part
-    out_ref[...] = total.astype(out_ref.dtype)
+    if packed:
+        store_packed(out_ref, total)
+    else:
+        out_ref[...] = total
 
 
 def finish_kernel(own_ref, received_ref, out_ref):
-    received = received_ref[...].astype(F32)
+    total = own_ref[...] + load_packed(received_ref, *own_ref.shape)
     for k in range(out_ref.shape[0]):
-        rows = slice(k * ROWS, (k + 1) * ROWS)
-        out_ref[k] = (own_ref[rows] + received[rows]).astype(BF16)
+        out_ref[k] = total[k * ROWS : (k + 1) * ROWS].astype(BF16)
 
 
 def vmem(count):
@@ -175,11 +208,12 @@
         cost_estimate=pl.CostEstimate(flops=2 * slots * row_count * SLOT * virtual, bytes_accessed=4 * slots * virtual, transcendentals=0),
         name="direct",
     )(direct)
-    amplitude = pl.pallas_call(
+    packed = jax.ShapeDtypeStruct((packed_height(rows, virtual)[-1], LANES), BF16)
+    ours, amplitude = pl.pallas_call(
         amplitude_kernel,
         in_specs=vmem(2),
-        out_specs=vmem(1)[0],
-        out_shape=jax.ShapeDtypeStruct((rows, virtual), BF16),
+        out_specs=vmem(2),
+        out_shape=[jax.ShapeDtypeStruct((rows, virtual), BF16), packed],
         scratch_shapes=[pltpu.VMEM((2, virtual, LANES), F32)],
         compiler_params=ROOM,
         name="amplitude",
@@ -187,12 +221,12 @@
 
     chunks = max(y_count // 2, 1)
 
-    def contraction(name, first, amplitude, dtype):
+    def contraction(name, first, amplitude, result):
         return pl.pallas_call(
-            functools.partial(contraction_kernel, orbitals=orbitals),
+            functools.partial(contraction_kernel, orbitals=orbitals, rows=rows, depth=virtual, packed=result is packed),
             in_specs=SMEM + vmem(1) + hbm(1),
             out_specs=vmem(1)[0],
-            out_shape=jax.ShapeDtypeStruct((rows, virtual), dtype),
+            out_shape=result,
             scratch_shapes=[pltpu.VMEM((y_count, 2 * half, lanes), BF16), pltpu.SemaphoreType.DMA((chunks,))],
             compiler_params=BIG,
             cost_estimate=pl.CostEstimate(flops=rows * virtual * block * y_count * 4, bytes_accessed=y_count * 4 * half * lanes, transcendentals=0),
@@ -202,8 +236,8 @@
     swap = [(0, 1), (1, 0)]
     partner = column + 1 - 2 * lax.axis_index("zh")
     theirs = lax.ppermute(amplitude, "zh", swap)
-    received = lax.ppermute(contraction("contraction_sent", partner * local, theirs, BF16), "zh", swap)
-    kept = contraction("contraction_kept", column * local, amplitude, F32)
+    received = lax.ppermute(contraction("contraction_sent", partner * local, theirs, packed), "zh", swap)
+    kept = contraction("contraction_kept", column * local, ours, jax.ShapeDtypeStruct((rows, virtual), F32))
     return pl.pallas_call(
         finish_kernel,
         in_specs=vmem(2),

time: 118 us -> 116 us (0.983)
  waiting for transfers between devices: 38.1 us -> 35.7 us
    ppermute x1, waiting for transfers between devices: 15.9 us -> 14.7 us  [body(): theirs = lax.ppermute(amplitude, 'zh', swap)]
where the time goes in v7:
time: 116 us
  waiting for transfers between devices  35.7 us (31%)
  blocking collectives  34.5 us (30%)
  starting transfers between devices  14.4 us (12%)
  Pallas kernels  13.7 us (12%)
  between operations  13.6 us (12%)
  local copies, waits for them, and re-layouts  3.69 us (3%)
    all_to_all x1, blocking collectives, body(): lax.all_to_all(pieces, ('y', 'zh'), 0, 0, tiled=True)  34.5 us
    ppermute x1, waiting for transfers between devices, body(): theirs = lax.ppermute(amplitude, 'zh', swap)  14.7 us
    ppermute x1, waiting for transfers between devices, body(): lax.ppermute(contraction('contraction_sent', partner * local, theirs, pac...  11.8 us
    all_to_all x1, starting transfers between devices, body(): mirrored = lax.all_to_all(direct, ('p', 'c'), 0, 0, tiled=True)  10.5 us
    all_to_all x1, waiting for transfers between devices, body(): mirrored = lax.all_to_all(direct, ('p', 'c'), 0, 0, tiled=True)  9.28 us
    pallas_call x2, Pallas kernels, contraction(): pl.pallas_call(functools.partial(contraction_kernel, orbitals=orbitals, r...  8.44 us
  transfers between devices with their start and end apart: 4, of which 3 were waited for; matrix products, arithmetic and copies ran while one was open for 3% of the time, Pallas kernels for 6%

profile of v7, /device:TPU:3, one launch (start us, length us, event | category | flops | bytes accessed | tf_op | source)
XLA Modules:
  0.0 115.8 jit_solution(462321489407339292)
XLA Ops:
  6.5 0.0 copy-start
  6.5 0.0 all-gather.2.cloned.1.call-start
  6.5 1.9 %pack.1 = bf16[848,256]{1,0:T(8,128)(2,1)} custom-call(s32[1]{0:T(128)} %bitcast.3.core_ref, bf16[800,250]{1,0:T(8,128)(2,1)} %bitcast.19, bf16[96,250]{1,0:T(8,128)(2,1)} %bitcast.21, bf16[800,250]{1,0:T(8,128)(2,1)} %bitcast.20), custom_call_target="tpu_custom_call" | custom-call | tf_op jit(solution)/shard_map/pack/pallas_call | solution.py:178
  8.4 0.0 all-gather.2.cloned.1.call-update
  8.5 0.0 copy-done
  8.5 0.4 copy.11
  8.8 0.5 reshape.25
  9.3 0.5 pad_slice_fusion
  9.8 0.2 copy.13
  10.0 0.2 reshape.27
  10.3 1.0 pad_slice_fusion.1
  11.2 0.4 copy.12
  11.6 0.4 reshape.26
  12.1 0.1 pad.13.clone
  12.1 0.2 fusion.6
  12.3 0.1 copy.14
  12.4 34.5 %all_to_all.10 = bf16[16,2,40,128]{3,2,1,0:T(8,128)(2,1)} all-to-all(bf16[16,2,40,128]{3,2,1,0:T(8,128)(2,1)S(1)} %copy.14), channel_id=1, replica_groups=mesh['p'=16,'c'=2,'y'=8,'zh'=2] {'y','zh'}, dimensions={0} | all-to-all | bytes 655360 | tf_op jit(solution)/shard_map/all_to_all | solution.py:198
  46.9 10.5 %all-to-all-start.1 = ((bf16[32,40,128]{2,1,0:T(8,128)(2,1)}), bf16[32,40,128]{2,1,0:T(8,128)(2,1)S(1)}, u32[]{:S(2)}, u32[]{:S(2)}) async-start(bf16[32,40,128]{2,1,0:T(8,128)(2,1)} %bitcast.2.pieces_ref), calls=%async_computation.1 | async-start | bytes 655360 | tf_op jit(solution)/shard_map/all_to_all | solution.py:199
  57.5 2.2 %direct.1.direct_ref = bf16[192,800]{1,0:T(8,128)(2,1)S(1)} custom-call(bf16[32,40,128]{2,1,0:T(8,128)(2,1)} %bitcast.2.pieces_ref), custom_call_target="tpu_custom_call" | custom-call | flops 314572800 | bytes 614400 | tf_op jit(solution)/shard_map/direct/pallas_call | solution.py:201
  59.7 9.3 %all-to-all-done.1.pieces_ref = bf16[32,40,128]{2,1,0:T(8,128)(2,1)S(1)} async-done(((bf16[32,40,128]{2,1,0:T(8,128)(2,1)}), bf16[32,40,128]{2,1,0:T(8,128)(2,1)S(1)}, u32[]{:S(2)}, u32[]{:S(2)}) %all-to-all-start.1) | async-done | bytes 327712 | tf_op jit(solution)/shard_map/all_to_all | solution.py:199
  69.0 0.3 amplitude.1
  69.3 1.9 %collective-permute-start = (bf16[952,128]{1,0:T(8,128)(2,1)S(1)}, bf16[952,128]{1,0:T(8,128)(2,1)S(1)}, u32[]{:S(2)}, u32[]{:S(2)}) collective-permute-start(bf16[952,128]{1,0:T(8,128)(2,1)S(1)} %get-tuple-element.8), channel_id=1, source_target_pairs={{0,1},{1,0},{2,3},{3,2},{4,5},{5,4},{6,7},{7,6},{8,9},{9,8},{10,11... | collective-permute-start | bytes 731144 | tf_op jit(solution)/shard_map/ppermute | solution.py:238
  71.2 14.7 %collective-permute-done.amplitude_ref = bf16[952,128]{1,0:T(8,128)(2,1)S(1)} collective-permute-done((bf16[952,128]{1,0:T(8,128)(2,1)S(1)}, bf16[952,128]{1,0:T(8,128)(2,1)S(1)}, u32[]{:S(2)}, u32[]{:S(2)}) %collective-permute-start) | collective-permute-done | bytes 243744 | tf_op jit(solution)/shard_map/ppermute | solution.py:238
  85.9 0.0 all-gather.2.cloned.1.call-done
  85.9 4.2 %contraction_sent.1 = bf16[952,128]{1,0:T(8,128)(2,1)S(1)} custom-call(s32[1]{0:T(128)} %bitcast.8.first_ref, bf16[952,128]{1,0:T(8,128)(2,1)S(1)} %collective-permute-done.amplitude_ref, bf16[8,1696,256]{2,1,0:T(8,128)(2,1)} %bitcast.15), custom_call_target="tpu_custom_call" | custom-call | flops 960000000 | bytes 6946816 | tf_op jit(solution)/shard_map/contraction_sent/pallas_call | solution.py:225
  90.1 1.9 %collective-permute-start.1 = (bf16[952,128]{1,0:T(8,128)(2,1)S(1)}, bf16[952,128]{1,0:T(8,128)(2,1)S(1)}, u32[]{:S(2)}, u32[]{:S(2)}) collective-permute-start(bf16[952,128]{1,0:T(8,128)(2,1)S(1)} %contraction_sent.1), channel_id=1, source_target_pairs={{0,1},{1,0},{2,3},{3,2},{4,5},{5,4},{6,7},{7,6},{8,9},{9,8},{10,11... | collective-permute-start | bytes 731144 | tf_op jit(solution)/shard_map/ppermute | solution.py:239
  92.1 4.2 %contraction_kept.1.own_ref = f32[150,800]{1,0:T(8,128)S(1)} custom-call(s32[1]{0:T(128)} %bitcast.first_ref, bf16[150,800]{1,0:T(8,128)(2,1)S(1)} %get-tuple-element.7.amplitude_ref, bf16[8,1696,256]{2,1,0:T(8,128)(2,1)} %bitcast.16), custom_call_target="tpu_custom_call" | custom-call | flops 960000000 | bytes 6946816 | tf_op jit(solution)/shard_map/contraction_kept/pallas_call | solution.py:225
  96.3 11.8 %collective-permute-done.1.received_ref = bf16[952,128]{1,0:T(8,128)(2,1)S(1)} collective-permute-done((bf16[952,128]{1,0:T(8,128)(2,1)S(1)}, bf16[952,128]{1,0:T(8,128)(2,1)S(1)}, u32[]{:S(2)}, u32[]{:S(2)}) %collective-permute-start.1) | collective-permute-done | bytes 243744 | tf_op jit(solution)/shard_map/ppermute | solution.py:239
  108.1 0.9 finish.1
  (3 shorter events, 0.0 us)
Async XLA Ops:
  6.5 1.9 %copy-start = (bf16[96,25,50]{0,2,1:T(8,128)(2,1)S(1)}, bf16[96,25,50]{0,2,1:T(8,128)(2,1)}, u32[]{:S(2)}) copy-start(bf16[96,25,50]{0,2,1:T(8,128)(2,1)} %param.4) | copy-start | bytes 720004
  6.5 79.3 %all-gather.2.cloned.1.call-start = ((), (), s32[]{:S(2)}) async-start(), calls=%async_computation.2 | async-start | bytes 7380992 | tf_op jit(solution)/shard_map/all_gather | solution.py:187
  46.9 22.0 %all-to-all-start.1 = ((bf16[32,40,128]{2,1,0:T(8,128)(2,1)}), bf16[32,40,128]{2,1,0:T(8,128)(2,1)S(1)}, u32[]{:S(2)}, u32[]{:S(2)}) async-start(bf16[32,40,128]{2,1,0:T(8,128)(2,1)} %bitcast.2.pieces_ref), calls=%async_computation.1 | async-start | bytes 655360 | tf_op jit(solution)/shard_map/all_to_all | solution.py:199
  69.3 16.6 %collective-permute-start = (bf16[952,128]{1,0:T(8,128)(2,1)S(1)}, bf16[952,128]{1,0:T(8,128)(2,1)S(1)}, u32[]{:S(2)}, u32[]{:S(2)}) collective-permute-start(bf16[952,128]{1,0:T(8,128)(2,1)S(1)} %get-tuple-element.8), channel_id=1, source_target_pairs={{0,1},{1,0},{2,3},{3,2},{4,5},{5,4},{6,7},{7,6},{8,9},{9,8},{10,11... | collective-permute-start | bytes 731144 | tf_op jit(solution)/shard_map/ppermute | solution.py:238
  90.1 17.9 %collective-permute-start.1 = (bf16[952,128]{1,0:T(8,128)(2,1)S(1)}, bf16[952,128]{1,0:T(8,128)(2,1)S(1)}, u32[]{:S(2)}, u32[]{:S(2)}) collective-permute-start(bf16[952,128]{1,0:T(8,128)(2,1)S(1)} %contraction_sent.1), channel_id=1, source_target_pairs={{0,1},{1,0},{2,3},{3,2},{4,5},{5,4},{6,7},{7,6},{8,9},{9,8},{10,11... | collective-permute-start | bytes 731144 | tf_op jit(solution)/shard_map/ppermute | solution.py:239
Sparse Core Ops, SparseCore 0:
  9.5 63.4 all-gather.1

commit v8 on v7

--- a/solution.py
+++ b/solution.py
@@ -112,22 +112,18 @@
     store_packed(packed_ref, value)
 
 
-def contraction_kernel(first_ref, amplitude_ref, factors_hbm, out_ref, held, sems, *, orbitals, rows, depth, packed):
-    chunks = sems.shape[0]
-    per = factors_hbm.shape[0] // chunks
-    copies = [
-        pltpu.make_async_copy(factors_hbm.at[pl.ds(j * per, per)], held.at[pl.ds(j * per, per)], sems.at[j])
-        for j in range(chunks)
-    ]
-    for copy in copies:
-        copy.start()
+def ready_kernel(held, out_ref):
+    out_ref[...] = held[0, :16, :LANES]
+
+
+def contraction_kernel(first_ref, amplitude_ref, held, ready_ref, out_ref, *, orbitals, rows, depth, packed, chunks):
+    per = held.shape[0] // chunks
     begin = (lax.broadcasted_iota(jnp.int32, (rows, orbitals), 1) - first_ref[0]) * ROWS
     row = lax.broadcasted_iota(jnp.int32, (rows, orbitals), 0)
     pick = jnp.where((row >= begin) & (row < begin + ROWS), 1.0, 0.0).astype(BF16)
     amplitude = load_packed(amplitude_ref, rows, depth).astype(BF16) if packed else amplitude_ref[...]
     total = None
     for j in range(chunks):
-        copies[j].wait()
         scaled, second = [], []
         for k in range(j * per, (j + 1) * per):
             value = jnp.dot(amplitude, held[k, :depth], preferred_element_type=F32)
@@ -161,7 +157,8 @@
 SMEM = [pl.BlockSpec(memory_space=pltpu.SMEM)]
 ROOM = pltpu.CompilerParams(vmem_limit_bytes=32 * 2**20)
 SMALL = pltpu.CompilerParams(vmem_limit_bytes=16 * 2**20)
-BIG = pltpu.CompilerParams(vmem_limit_bytes=48 * 2**20)
+BIG = pltpu.CompilerParams(vmem_limit_bytes=32 * 2**20)
+FETCH = pltpu.CompilerParams(vmem_limit_bytes=32 * 2**20)
 FULL = pltpu.CompilerParams(vmem_limit_bytes=60 * 2**20)
 
 
@@ -219,19 +216,28 @@
         name="amplitude",
     )(direct, mirrored)
 
-    chunks = max(y_count // 2, 1)
+    ready = pl.pallas_call(
+        ready_kernel,
+        in_specs=vmem(1),
+        out_specs=vmem(1)[0],
+        out_shape=jax.ShapeDtypeStruct((16, LANES), BF16),
+        compiler_params=FETCH,
+        cost_estimate=pl.CostEstimate(flops=0, bytes_accessed=2 * factors.size, transcendentals=0),
+        name="ready",
+    )(factors)
 
     def contraction(name, first, amplitude, result):
         return pl.pallas_call(
-            functools.partial(contraction_kernel, orbitals=orbitals, rows=rows, depth=virtual, packed=result is packed),
-            in_specs=SMEM + vmem(1) + hbm(1),
+            functools.partial(
+                contraction_kernel, orbitals=orbitals, rows=rows, depth=virtual, packed=result is packed, chunks=max(y_count // 2, 1)
+            ),
+            in_specs=SMEM + vmem(3),
             out_specs=vmem(1)[0],
             out_shape=result,
-            scratch_shapes=[pltpu.VMEM((y_count, 2 * half, lanes), BF16), pltpu.SemaphoreType.DMA((chunks,))],
             compiler_params=BIG,
             cost_estimate=pl.CostEstimate(flops=rows * virtual * block * y_count * 4, bytes_accessed=y_count * 4 * half * lanes, transcendentals=0),
             name=name,
-        )(first.reshape(1), amplitude, factors)
+        )(first.reshape(1), amplitude, factors, ready)
 
     swap = [(0, 1), (1, 0)]
     partner = column + 1 - 2 * lax.axis_index("zh")

time: 116 us -> 114 us (0.983)
  local copies, waits for them, and re-layouts: 3.69 us -> 9.62 us
  waiting for transfers between devices: 35.7 us -> 31.7 us
  Pallas kernels: 13.7 us -> 9.89 us
    unnamed x3 -> x7, local copies, waits for them, and re-layouts: 0.36 us -> 6.3 us
    ppermute x1, waiting for transfers between devices: 14.7 us -> 9.97 us  [body(): theirs = lax.ppermute(amplitude, 'zh', swap)]
    pallas_call x2, Pallas kernels: 8.44 us -> 4.59 us  [contraction(): pl.pallas_call(functools.partial(contraction_kernel, orbitals=orbitals, r...]
    all_gather x1, waiting for transfers between devices: 0.01 us -> 1.71 us  [body(): lax.all_gather(share, ('y', 'c'), axis=0, tiled=True)]
  transfers between devices with their start and end apart: 4 -> 4, of which waited for: 3 -> 4; matrix products, arithmetic and copies ran while one was open for 3% -> 3% of each run, Pallas kernels for 6% -> 4%
where the time goes in v8:
time: 114 us
  blocking collectives  34.5 us (30%)
  waiting for transfers between devices  31.7 us (28%)
  starting transfers between devices  14.4 us (13%)
  between operations  13.6 us (12%)
  Pallas kernels  9.89 us (9%)
  local copies, waits for them, and re-layouts  9.62 us (8%)
    all_to_all x1, blocking collectives, body(): lax.all_to_all(pieces, ('y', 'zh'), 0, 0, tiled=True)  34.5 us
    ppermute x1, waiting for transfers between devices, body(): lax.ppermute(contraction('contraction_sent', partner * local, theirs, pac...  10.7 us
    all_to_all x1, starting transfers between devices, body(): mirrored = lax.all_to_all(direct, ('p', 'c'), 0, 0, tiled=True)  10.5 us
    ppermute x1, waiting for transfers between devices, body(): theirs = lax.ppermute(amplitude, 'zh', swap)  9.97 us
    all_to_all x1, waiting for transfers between devices, body(): mirrored = lax.all_to_all(direct, ('p', 'c'), 0, 0, tiled=True)  9.26 us
    unnamed x7, local copies, waits for them, and re-layouts  6.3 us
    pallas_call x2, Pallas kernels, contraction(): pl.pallas_call(functools.partial(contraction_kernel, orbitals=orbitals, r...  4.59 us
  transfers between devices with their start and end apart: 4, of which 4 were waited for; matrix products, arithmetic and copies ran while one was open for 3% of the time, Pallas kernels for 4%

profile of v8, /device:TPU:3, one launch (start us, length us, event | category | flops | bytes accessed | tf_op | source)
XLA Modules:
  0.0 113.8 jit_solution(2295956837880806971)
XLA Ops:
  6.5 0.0 copy-start.2
  6.5 0.0 all-gather.2.cloned.1.call-start
  6.5 1.9 %pack.1 = bf16[848,256]{1,0:T(8,128)(2,1)} custom-call(s32[1]{0:T(128)} %bitcast.3.core_ref, bf16[800,250]{1,0:T(8,128)(2,1)} %bitcast.20, bf16[96,250]{1,0:T(8,128)(2,1)} %bitcast.22, bf16[800,250]{1,0:T(8,128)(2,1)} %bitcast.21), custom_call_target="tpu_custom_call" | custom-call | tf_op jit(solution)/shard_map/pack/pallas_call | solution.py:175
  8.4 0.0 all-gather.2.cloned.1.call-update
  8.5 0.0 copy-done.2
  8.5 0.4 copy.11
  8.8 0.5 reshape.25
  9.3 0.5 pad_slice_fusion
  9.8 0.2 copy.13
  10.0 0.2 reshape.27
  10.3 1.0 pad_slice_fusion.1
  11.2 0.4 copy.12
  11.6 0.4 reshape.26
  12.1 0.1 pad.13.clone
  12.1 0.2 fusion.6
  12.3 0.1 copy.14
  12.4 34.5 %all_to_all.10 = bf16[16,2,40,128]{3,2,1,0:T(8,128)(2,1)} all-to-all(bf16[16,2,40,128]{3,2,1,0:T(8,128)(2,1)S(1)} %copy.14), channel_id=1, replica_groups=mesh['p'=16,'c'=2,'y'=8,'zh'=2] {'y','zh'}, dimensions={0} | all-to-all | bytes 655360 | tf_op jit(solution)/shard_map/all_to_all | solution.py:195
  46.9 10.5 %all-to-all-start.1 = ((bf16[32,40,128]{2,1,0:T(8,128)(2,1)}), bf16[32,40,128]{2,1,0:T(8,128)(2,1)S(1)}, u32[]{:S(2)}, u32[]{:S(2)}) async-start(bf16[32,40,128]{2,1,0:T(8,128)(2,1)} %bitcast.2.pieces_ref), calls=%async_computation.1 | async-start | bytes 655360 | tf_op jit(solution)/shard_map/all_to_all | solution.py:196
  57.5 2.2 %direct.1.direct_ref = bf16[192,800]{1,0:T(8,128)(2,1)S(1)} custom-call(bf16[32,40,128]{2,1,0:T(8,128)(2,1)} %bitcast.2.pieces_ref), custom_call_target="tpu_custom_call" | custom-call | flops 314572800 | bytes 614400 | tf_op jit(solution)/shard_map/direct/pallas_call | solution.py:198
  59.7 9.3 %all-to-all-done.1.pieces_ref = bf16[32,40,128]{2,1,0:T(8,128)(2,1)S(1)} async-done(((bf16[32,40,128]{2,1,0:T(8,128)(2,1)}), bf16[32,40,128]{2,1,0:T(8,128)(2,1)S(1)}, u32[]{:S(2)}, u32[]{:S(2)}) %all-to-all-start.1) | async-done | bytes 327712 | tf_op jit(solution)/shard_map/all_to_all | solution.py:196
  69.0 0.3 amplitude.1
  69.3 1.9 %collective-permute-start = (bf16[952,128]{1,0:T(8,128)(2,1)S(1)}, bf16[952,128]{1,0:T(8,128)(2,1)S(1)}, u32[]{:S(2)}, u32[]{:S(2)}) collective-permute-start(bf16[952,128]{1,0:T(8,128)(2,1)S(1)} %get-tuple-element.8), channel_id=1, source_target_pairs={{0,1},{1,0},{2,3},{3,2},{4,5},{5,4},{6,7},{7,6},{8,9},{9,8},{10,11... | collective-permute-start | bytes 731144 | tf_op jit(solution)/shard_map/ppermute | solution.py:244
  71.2 1.7 %all-gather.2.cloned.1.call-done = bf16[13568,256]{1,0:T(8,128)(2,1)} async-done(((bf16[848,256]{1,0:T(8,128)(2,1)}), bf16[13568,256]{1,0:T(8,128)(2,1)}) %all-gather.2.cloned.1.call-update) | async-done | bytes 6946832 | tf_op jit(solution)/shard_map/all_gather | solution.py:184
  72.9 0.0 copy-start
  72.9 3.0 %copy-done = bf16[13568,256]{1,0:T(8,128)(2,1)S(1)} copy-done((bf16[13568,256]{1,0:T(8,128)(2,1)S(1)}, bf16[13568,256]{1,0:T(8,128)(2,1)}, u32[]{:S(2)}) %copy-start) | copy-done | bytes 6946840
  75.9 10.0 %collective-permute-done.amplitude_ref = bf16[952,128]{1,0:T(8,128)(2,1)S(1)} collective-permute-done((bf16[952,128]{1,0:T(8,128)(2,1)S(1)}, bf16[952,128]{1,0:T(8,128)(2,1)S(1)}, u32[]{:S(2)}, u32[]{:S(2)}) %collective-permute-start) | collective-permute-done | bytes 243744 | tf_op jit(solution)/shard_map/ppermute | solution.py:244
  85.9 2.3 %contraction_sent.1 = bf16[952,128]{1,0:T(8,128)(2,1)S(1)} custom-call(s32[1]{0:T(128)} %bitcast.8.first_ref, bf16[952,128]{1,0:T(8,128)(2,1)S(1)} %collective-permute-done.amplitude_ref, bf16[8,1696,256]{2,1,0:T(8,128)(2,1)S(1)} %bitcast.16, bf16[16,128]{1,0:T(8,128)(2,1)S(1)} %ready.1.ready_ref), custom_call_target="tpu_custom_call" | custom-call | flops 960000000 | bytes 6946816 | tf_op jit(solution)/shard_map/contraction_sent/pallas_call | solution.py:230
  88.2 1.9 %collective-permute-start.1 = (bf16[952,128]{1,0:T(8,128)(2,1)S(1)}, bf16[952,128]{1,0:T(8,128)(2,1)S(1)}, u32[]{:S(2)}, u32[]{:S(2)}) collective-permute-start(bf16[952,128]{1,0:T(8,128)(2,1)S(1)} %contraction_sent.1), channel_id=1, source_target_pairs={{0,1},{1,0},{2,3},{3,2},{4,5},{5,4},{6,7},{7,6},{8,9},{9,8},{10,11... | collective-permute-start | bytes 731144 | tf_op jit(solution)/shard_map/ppermute | solution.py:245
  90.1 0.0 copy-start.1
  90.1 3.0 %copy-done.1 = bf16[13568,256]{1,0:T(8,128)(2,1)S(1)} copy-done((bf16[13568,256]{1,0:T(8,128)(2,1)S(1)}, bf16[13568,256]{1,0:T(8,128)(2,1)}, u32[]{:S(2)}) %copy-start.1) | copy-done | bytes 6946840
  93.1 2.3 %contraction_kept.1.own_ref = f32[150,800]{1,0:T(8,128)S(1)} custom-call(s32[1]{0:T(128)} %bitcast.first_ref, bf16[150,800]{1,0:T(8,128)(2,1)S(1)} %get-tuple-element.7.amplitude_ref, bf16[8,1696,256]{2,1,0:T(8,128)(2,1)S(1)} %bitcast.17, bf16[16,128]{1,0:T(8,128)(2,1)S(1)} %ready.1.ready_ref), custom_call_target="tpu_custom_call" | custom-call | flops 960000000 | bytes 6946816 | tf_op jit(solution)/shard_map/contraction_kept/pallas_call | solution.py:230
  95.4 10.7 %collective-permute-done.1.received_ref = bf16[952,128]{1,0:T(8,128)(2,1)S(1)} collective-permute-done((bf16[952,128]{1,0:T(8,128)(2,1)S(1)}, bf16[952,128]{1,0:T(8,128)(2,1)S(1)}, u32[]{:S(2)}, u32[]{:S(2)}) %collective-permute-start.1) | collective-permute-done | bytes 243744 | tf_op jit(solution)/shard_map/ppermute | solution.py:245
  106.1 0.9 finish.1
  (4 shorter events, 0.0 us)
Async XLA Ops:
  6.5 1.9 %copy-start.2 = (bf16[96,25,50]{0,2,1:T(8,128)(2,1)S(1)}, bf16[96,25,50]{0,2,1:T(8,128)(2,1)}, u32[]{:S(2)}) copy-start(bf16[96,25,50]{0,2,1:T(8,128)(2,1)} %param.4) | copy-start | bytes 720004
  6.5 66.4 %all-gather.2.cloned.1.call-start = ((), (), s32[]{:S(2)}) async-start(), calls=%async_computation.2 | async-start | bytes 7380992 | tf_op jit(solution)/shard_map/all_gather | solution.py:184
  46.9 22.0 %all-to-all-start.1 = ((bf16[32,40,128]{2,1,0:T(8,128)(2,1)}), bf16[32,40,128]{2,1,0:T(8,128)(2,1)S(1)}, u32[]{:S(2)}, u32[]{:S(2)}) async-start(bf16[32,40,128]{2,1,0:T(8,128)(2,1)} %bitcast.2.pieces_ref), calls=%async_computation.1 | async-start | bytes 655360 | tf_op jit(solution)/shard_map/all_to_all | solution.py:196
  69.3 16.6 %collective-permute-start = (bf16[952,128]{1,0:T(8,128)(2,1)S(1)}, bf16[952,128]{1,0:T(8,128)(2,1)S(1)}, u32[]{:S(2)}, u32[]{:S(2)}) collective-permute-start(bf16[952,128]{1,0:T(8,128)(2,1)S(1)} %get-tuple-element.8), channel_id=1, source_target_pairs={{0,1},{1,0},{2,3},{3,2},{4,5},{5,4},{6,7},{7,6},{8,9},{9,8},{10,11... | collective-permute-start | bytes 731144 | tf_op jit(solution)/shard_map/ppermute | solution.py:244
  72.9 3.0 %copy-start = (bf16[13568,256]{1,0:T(8,128)(2,1)S(1)}, bf16[13568,256]{1,0:T(8,128)(2,1)}, u32[]{:S(2)}) copy-start(bf16[13568,256]{1,0:T(8,128)(2,1)} %all-gather.2.cloned.1.call-done) | copy-start | bytes 20840452
  88.2 17.9 %collective-permute-start.1 = (bf16[952,128]{1,0:T(8,128)(2,1)S(1)}, bf16[952,128]{1,0:T(8,128)(2,1)S(1)}, u32[]{:S(2)}, u32[]{:S(2)}) collective-permute-start(bf16[952,128]{1,0:T(8,128)(2,1)S(1)} %contraction_sent.1), channel_id=1, source_target_pairs={{0,1},{1,0},{2,3},{3,2},{4,5},{5,4},{6,7},{7,6},{8,9},{9,8},{10,11... | collective-permute-start | bytes 731144 | tf_op jit(solution)/shard_map/ppermute | solution.py:245
  90.1 3.0 %copy-start.1 = (bf16[13568,256]{1,0:T(8,128)(2,1)S(1)}, bf16[13568,256]{1,0:T(8,128)(2,1)}, u32[]{:S(2)}) copy-start(bf16[13568,256]{1,0:T(8,128)(2,1)} %all-gather.2.cloned.1.call-done) | copy-start | bytes 20840452
Sparse Core Ops, SparseCore 0:
  9.5 63.4 all-gather.1
